TPU v7x, 256 devices: a whole 4x4x8 slice. The times are simulated.
256 devices in a mesh: segment: 4 (over x), seq: 16 (over z, y_hi), mp: 4 (over y_lo, core).
Axes of the slice: x: 4, y: 4 (y_hi: 2, y_lo: 2; y = y_hi * 2 + y_lo), z: 8, core: 2. Of those that a mesh axis runs over, the one named last changes fastest.
Arguments:
- captions: bfloat16 [16, 128, 4096], P('seq', None, 'segment'), may hold values from -6 to 6
- caption_lengths: int32 [16], replicated, may hold values from 1 to 128, as said below
- image_caption: int32 [16], replicated, may hold values from 0 to 15, each once
- t5_gain: float32 [4096], P('segment'), may hold values from 0.25 to 1.75
- w_key: bfloat16 [4096, 4096], P('segment', 'mp'), may hold values from -0.09375 to 0.09375
- w_value: bfloat16 [4096, 4096], P('segment', 'mp'), may hold values from -0.09375 to 0.09375
- queries: bfloat16 [16, 4096, 4096], P('segment', 'seq', 'mp'), may hold values from -300 to 300
- hidden: bfloat16 [16, 4096, 4096], P('segment', 'seq', 'mp'), may hold values from -1.5 to 1.5
- out_gate: float32 [16, 4096], P('segment', 'mp'), may hold values from 1 to 4
- w_out: bfloat16 [4096, 4096], P('mp', 'seq'), may hold values from -0.09375 to 0.09375
Outputs:
- result_rows: bfloat16 [16, 4096, 4096], P('segment', 'seq', 'mp')
Inputs may be any that keep to these rules, and one draw needn't show every extreme that they name: `caption_lengths`: each caption has at least one live token, and some caption fills all 128 slots.
All inputs are finite; a program needn't handle non-finite values.
Results may differ from a plain program's by a relative error of at most 0.03.
Values may be sent and summed in bfloat16 or wider, within the bound.
No kernel may reach another device: no remote copies, remote signals or barrier semaphores. Data moves between devices by JAX's collectives and lax.ppermute only.
A program may use at most 128 MiB of HBM per device.

v0:
```python
import functools
import math

import jax
import jax.numpy as jnp
from jax import lax
from jax.experimental import pallas as pl
from jax.experimental.pallas import tpu as pltpu
from jax.sharding import Mesh
from jax.sharding import PartitionSpec as P

HEAD = 128
SEQ = ("z", "yh")
MP = ("yl", "core")
SWAP = [(0, 1), (1, 0)]
VMEM = pl.BlockSpec(memory_space=pltpu.VMEM)
SMEM = pl.BlockSpec(memory_space=pltpu.SMEM)
PARAMS = pltpu.CompilerParams(vmem_limit_bytes=26 * 1024 * 1024)
F32 = jnp.float32
BF16 = jnp.bfloat16


def rotation(count, by):
    return [(k, (k + by) % count) for k in range(count)]


def after(value, *tokens):
    return lax.optimization_barrier((value, *tokens))[0]


def cost(flops, moved):
    return pl.CostEstimate(flops=flops, bytes_accessed=moved, transcendentals=0)


def ring_of(value, count, *beside):
    half = count // 2
    ring = [value] + [None] * (count - 1)
    for k in range(1, half + 1):
        if k == half:
            ring[k - 1] = after(ring[k - 1], *beside)
        ring[k] = lax.ppermute(ring[k - 1], "z", rotation(count, 1))
        if k < half:
            ring[count - k] = lax.ppermute(ring[(count - k + 1) % count], "z", rotation(count, -1))
    return ring


def project_kernel(nx, owner_ref, pieces_ref, gain_ref, wk_ref, wv_ref, *rest):
    outs, (scaled, scratch) = rest[:nx], rest[nx:]
    captions, slots, share = pieces_ref.shape
    step, steps = pl.program_id(0), pl.num_programs(0)
    block = wk_ref.shape[1]
    cols = (scratch.shape[1] - HEAD) // 2

    @pl.when(step == 0)
    def _():
        rows = pieces_ref[...].reshape(captions * slots, share).astype(F32)
        squares = jnp.sum(rows * rows, axis=1, keepdims=True)
        high = squares.astype(BF16).astype(F32)
        low = squares - high
        lane = lax.broadcasted_iota(jnp.int32, (captions * slots, HEAD), 1)
        tail = jnp.where(lane == 0, high, jnp.where(lane == 1, low, 0.0))
        scratch[:, 2 * cols :] = tail.astype(BF16)
        scaled[...] = (rows * gain_ref[...]).astype(BF16)

    for ref, offset in ((wk_ref, 0), (wv_ref, cols)):
        at = pl.ds(pl.multiple_of(offset + step * block, block), block)
        scratch[:, at] = jnp.dot(scaled[...], ref[...], preferred_element_type=F32).astype(BF16)

    @pl.when(step == steps - 1)
    def _():
        x = lax.axis_index("x")
        images = outs[0].shape[0]
        for r in range(nx):
            there = lax.rem(x + r, nx)
            for j in range(images):
                caption = owner_ref[there * images + j]
                start = pl.multiple_of(caption * slots, slots)
                outs[r][j] = scratch[pl.ds(start, slots), :]


def add_kernel(width, *refs):
    parts, out_ref = refs[:-1], refs[-1]
    wide = parts[0].shape[2]
    cols = (wide - HEAD) // 2
    total = parts[0][...].astype(F32)
    for p in parts[1:]:
        total = total + p[...].astype(F32)
    squares = total[:, :, 2 * cols : 2 * cols + 1] + total[:, :, 2 * cols + 1 : 2 * cols + 2]
    scale = lax.rsqrt(squares / width + 1e-06)
    keys = total[:, :, :cols] * (scale * (HEAD**-0.5 * math.log2(math.e)))
    out_ref[:, :, :cols] = keys.astype(BF16)
    out_ref[:, :, cols:] = (total[:, :, cols : 2 * cols] * scale).astype(BF16)


def attend_kernel(first, total, nz, owner_ref, length_ref, mine_ref, theirs_ref, *rest):
    pieces, (keep_ref, send_ref) = rest[:nz], rest[nz:]
    core, z = lax.axis_index("core"), lax.axis_index("z")
    rows, cols = mine_ref.shape[1:]
    slots = pieces[0].shape[1]
    image = lax.axis_index("x") * total + first + pl.program_id(0)
    live = length_ref[owner_ref[image]]
    lane = lax.broadcasted_iota(jnp.int32, (2 * rows, HEAD), 1)
    slot = lax.rem(z + nz - lane // slots, nz) * slots + lax.rem(lane, slots)
    dead = slot >= live

    for h in range(cols // HEAD):
        at = slice(h * HEAD, (h + 1) * HEAD)
        there = slice(cols + h * HEAD, cols + (h + 1) * HEAD)
        mine, theirs = mine_ref[0, :, at], theirs_ref[0, :, at]
        q = jnp.concatenate(
            [jnp.where(core == 0, mine, theirs), jnp.where(core == 0, theirs, mine)], axis=0
        )
        keys = jnp.concatenate([p[0, :, at] for p in pieces], axis=0)
        values = jnp.concatenate([p[0, :, there] for p in pieces], axis=0)
        scores = lax.dot_general(q, keys, (((1,), (1,)), ((), ())), preferred_element_type=F32)
        scores = jnp.where(dead, -1e30, scores)
        top = jnp.max(scores, axis=1, keepdims=True)
        raised = jnp.exp2(scores - top)
        weights = (raised / jnp.sum(raised, axis=1, keepdims=True)).astype(BF16)
        out = jnp.dot(weights, values, preferred_element_type=F32).astype(BF16)
        keep_ref[:, at] = out[:rows]
        send_ref[:, at] = out[rows:]


def output_kernel(nx, nz, order_ref, keep_ref, come_ref, *rest):
    sides, outs, (held, sems) = (rest[:5], rest[5:10]), rest[10:-2], rest[-2:]
    sends, stays = outs[: len(outs) // 2], outs[len(outs) // 2 :]
    x = lax.axis_index("x")
    core, yl = lax.axis_index("core"), lax.axis_index("yl")
    deep, wide = rest[0].shape[1:]
    sent_block = jnp.where(core == 0, 1 - yl, yl)
    half = nz // 2

    copies = []
    for first in range(2):
        span = pl.ds(first * half, half)
        group = []
        for side in range(2):
            for part in range(nx):
                ref = sides[side][part].at[span] if part < nx - 1 else sides[side][part + first]
                row = pl.ds((side * nx + part) * deep, deep)
                group.append(
                    pltpu.make_async_copy(ref, held.at[span, row], sems.at[first, side, part])
                )
        copies.append(group)
    for group in copies:
        for copy in group:
            copy.start()

    slabs = []
    for ref in (keep_ref, come_ref):
        for r in (0, 1, nx - 1, 2):
            start = pl.multiple_of(lax.rem(x + nx - r, nx) * deep, deep)
            slabs.append(ref[:, pl.ds(start, deep)])
    left = jnp.concatenate(slabs, axis=1)

    def column(k):
        out = jnp.dot(left, held[k], preferred_element_type=F32).astype(BF16)
        there = k
        start = pl.multiple_of(lax.rem(there, half) * wide, wide)

        rows = sends[0].shape[0]

        @pl.when(there // half == sent_block)
        def _():
            for i, ref in enumerate(sends):
                ref[:, pl.ds(start, wide)] = out[i * rows : (i + 1) * rows]

        @pl.when(there // half != sent_block)
        def _():
            for i, ref in enumerate(stays):
                ref[:, pl.ds(start, wide)] = out[i * rows : (i + 1) * rows]

    for first in range(2):
        for copy in copies[first]:
            copy.wait()

        @pl.loop(0, half)
        def _(k):
            column(first * half + k)


def combine_kernel(stay_ref, come_ref, a_ref, b_ref):
    core = lax.axis_index("core")
    half = a_ref.shape[1]
    for ref, which in ((a_ref, 1 - core), (b_ref, core)):
        at = pl.ds(pl.multiple_of(which * half, half), half)
        ref[...] = (stay_ref[:, at].astype(F32) + come_ref[:, at].astype(F32)).astype(BF16)


def finish_kernel(image, hidden_ref, gate_ref, a_ref, b_ref, *rest):
    out_ref = rest[-1]
    core, yh = lax.axis_index("core"), lax.axis_index("yh")
    second = lax.rem(yh + core, 2)
    wide = a_ref.shape[1] // 2
    for ref, parity in ((a_ref, 1 - second), (b_ref, second)):
        for k in range(2):
            at = pl.ds(pl.multiple_of((2 * k + parity) * wide, wide), wide)
            part = ref[:, k * wide : (k + 1) * wide].astype(F32)
            out = hidden_ref[0, :, at].astype(F32) + gate_ref[image : image + 1, at] * part
            out_ref[0, :, at] = out.astype(BF16)


def shards(
    captions,
    caption_lengths,
    image_caption,
    t5_gain,
    w_key,
    w_value,
    queries,
    hidden,
    out_gate,
    w_out,
):
    nx, nz, nh = lax.axis_size("x"), lax.axis_size("z"), lax.axis_size("yh")
    _, slots, share = captions.shape
    images, rows, cols = queries.shape
    deep, wide = w_out.shape
    slot_share = slots // nz
    caption_count = nz * nh

    cut = captions.reshape(nz, 1, slot_share, share)
    cut = jnp.broadcast_to(cut, (nz, nh, slot_share, share))
    cut = cut.reshape(caption_count, slot_share, share)
    pieces = lax.all_to_all(cut, SEQ, 0, 0, tiled=True)

    theirs = lax.ppermute(after(queries, cut), "yh", SWAP)
    quarter = deep // nx
    mine = lax.dynamic_slice_in_dim(
        after(w_out, cut), lax.axis_index("x") * quarter, quarter, 0
    )
    w_z = lax.all_to_all(
        jnp.broadcast_to(mine[None], (nz, *mine.shape)), "z", 0, 0, tiled=True
    )

    partial = pl.pallas_call(
        functools.partial(project_kernel, nx),
        name="project",
        grid=(4,),
        out_shape=[jax.ShapeDtypeStruct((images, slot_share, 2 * cols + HEAD), BF16)] * nx,
        in_specs=[
            SMEM,
            pl.BlockSpec(pieces.shape, lambda i: (0, 0, 0)),
            pl.BlockSpec((1, share), lambda i: (0, 0)),
            pl.BlockSpec((share, cols // 4), lambda i: (0, i)),
            pl.BlockSpec((share, cols // 4), lambda i: (0, i)),
        ],
        out_specs=[
            pl.BlockSpec((images, slot_share, 2 * cols + HEAD), lambda i: (0, 0, 0))
        ]
        * nx,
        scratch_shapes=[
            pltpu.VMEM((caption_count * slot_share, share), BF16),
            pltpu.VMEM((caption_count * slot_share, 2 * cols + HEAD), BF16),
        ],
        compiler_params=pltpu.CompilerParams(vmem_limit_bytes=58 * 1024 * 1024),
        cost_estimate=cost(4 * caption_count * slot_share * share * cols, 6 << 20),
    )(image_caption, pieces, t5_gain.reshape(1, share), w_key, w_value)
    arrived = [partial[0]] + [
        lax.ppermute(partial[r], "x", rotation(nx, r)) for r in range(1, nx)
    ]
    stream = pl.pallas_call(
        functools.partial(add_kernel, float(share * nx)),
        name="add",
        out_shape=jax.ShapeDtypeStruct((images, slot_share, 2 * cols), BF16),
        in_specs=[VMEM] * nx,
        out_specs=VMEM,
        compiler_params=PARAMS,
        cost_estimate=cost(1 << 16, 1 << 16),
    )(*arrived)
    w_x = after(w_z, stream)
    ahead = lax.ppermute(w_x, "x", rotation(nx, 1))
    back = lax.ppermute(w_x, "x", rotation(nx, -1))
    ring = ring_of(stream, nz, ahead, back)
    far = [
        lax.ppermute(ahead[: nz // 2], "x", rotation(nx, 1)),
        lax.ppermute(back[nz // 2 :], "x", rotation(nx, -1)),
    ]
    w_mine = [w_x, ahead, back, *far]
    w_theirs = [lax.ppermute(w, "core", SWAP) for w in w_mine]

    across = [(h * 4 + l * 2, h * 4 + l * 2 + 1) for h in range(2) for l in range(2)]
    across += [(h * 4 + l * 2 + 1, (1 - h) * 4 + (1 - l) * 2) for h in range(2) for l in range(2)]
    beside = [(h * 4 + l * 2, h * 4 + l * 2) for h in range(2) for l in range(2)]
    beside += [
        (h * 4 + l * 2 + 1, (1 - h) * 4 + (1 - l) * 2 + 1) for h in range(2) for l in range(2)
    ]

    result = None
    batch = images // 2
    for s in range(2):
        block = pl.BlockSpec((1, rows, cols), lambda i, s=s: (s * batch + i, 0, 0))
        piece = pl.BlockSpec((1, slot_share, 2 * cols), lambda i, s=s: (s * batch + i, 0, 0))
        flat = pl.BlockSpec((rows, cols), lambda i: (i, 0))
        keep, send = pl.pallas_call(
            functools.partial(attend_kernel, s * batch, images, nz),
            name="attend",
            grid=(batch,),
            out_shape=[jax.ShapeDtypeStruct((batch * rows, cols), BF16)] * 2,
            in_specs=[SMEM, SMEM, block, block] + [piece] * nz,
            out_specs=[flat, flat],
            compiler_params=PARAMS,
            cost_estimate=cost(1 << 16, 1 << 16),
        )(
            after(image_caption, *far) if s else image_caption,
            caption_lengths,
            queries,
            theirs,
            *ring,
        )
        come = lax.ppermute(send, "core", SWAP)
        outs = pl.pallas_call(
            functools.partial(output_kernel, nx, nz),
            name="output",
            out_shape=[jax.ShapeDtypeStruct((rows, nz // 2 * wide), BF16)] * (2 * batch),
            in_specs=[SMEM, VMEM, VMEM] + [pl.BlockSpec(memory_space=pl.ANY)] * 10,
            out_specs=[VMEM] * (2 * batch),
            scratch_shapes=[
                pltpu.VMEM((nz, 2 * deep, wide), BF16),
                pltpu.SemaphoreType.DMA((2, 2, nx)),
            ],
            compiler_params=PARAMS,
            cost_estimate=cost(1 << 16, 1 << 16),
        )(image_caption, keep, come, *w_mine, *w_theirs)
        for i in range(batch):
            j = s * batch + i
            out_come = lax.ppermute(outs[i], "yl", SWAP)
            a, b = pl.pallas_call(
                combine_kernel,
                name="combine",
                out_shape=[jax.ShapeDtypeStruct((rows, cols // 2), BF16)] * 2,
                in_specs=[VMEM] * 2,
                out_specs=[VMEM] * 2,
                compiler_params=PARAMS,
                cost_estimate=cost(1 << 16, 1 << 16),
            )(outs[batch + i], out_come)
            a = lax.ppermute(a, ("yh", "yl", "core"), across)
            b = lax.ppermute(b, ("yh", "yl", "core"), beside)
            before = [] if result is None else [result]
            part = pl.BlockSpec((rows, cols // 2), lambda i: (0, 0))
            block = pl.BlockSpec((1, rows, cols), lambda i, j=j: (j, 0, 0))
            result = pl.pallas_call(
                functools.partial(finish_kernel, j),
                name="finish",
                grid=(1,),
                out_shape=jax.ShapeDtypeStruct(hidden.shape, BF16),
                in_specs=[block, pl.BlockSpec(out_gate.shape, lambda i: (0, 0)), part, part]
                + [pl.BlockSpec(memory_space=pl.ANY)] * len(before),
                out_specs=block,
                input_output_aliases={4: 0} if before else {},
                compiler_params=PARAMS,
                cost_estimate=cost(1 << 16, 1 << 16),
            )(hidden, out_gate, a, b, *before)
    return result


def solution(mesh):
    split = Mesh(
        mesh.devices.reshape(mesh.shape["segment"], 8, 2, 2, 2), ("x", "z", "yh", "yl", "core")
    )
    return jax.shard_map(
        shards,
        mesh=split,
        in_specs=(
            P(SEQ, None, "x"),
            P(),
            P(),
            P("x"),
            P("x", MP),
            P("x", MP),
            P("x", SEQ, MP),
            P("x", SEQ, MP),
            P("x", MP),
            P(MP, SEQ),
        ),
        out_specs=P("x", SEQ, MP),
        check_vma=False,
    )
```

profile of v0, /device:TPU:1, one launch (start us, length us, event | category | flops | bytes accessed | tf_op | source)
XLA Modules:
  0.0 193.7 jit_solution(14590072527459845094)
XLA Ops:
  1.9 11.7 %all-to-all-start.1 = ((bf16[16,16,1024]{2,1,0:T(8,128)(2,1)}), bf16[16,16,1024]{2,1,0:T(8,128)(2,1)S(1)}, u32[]{:S(2)}, u32[]{:S(2)}) async-start(bf16[16,16,1024]{2,1,0:T(8,128)(2,1)} %bitcast.1), calls=%async_computation.1 | async-start | bytes 1048576 | tf_op jit(solution)/shard_map/all_to_all | solution.py:226
  13.7 17.1 %all-to-all-done.1.pieces_ref = bf16[16,16,1024]{2,1,0:T(8,128)(2,1)S(1)} async-done(((bf16[16,16,1024]{2,1,0:T(8,128)(2,1)}), bf16[16,16,1024]{2,1,0:T(8,128)(2,1)S(1)}, u32[]{:S(2)}, u32[]{:S(2)}) %all-to-all-start.1) | async-done | bytes 524320 | tf_op jit(solution)/shard_map/all_to_all | solution.py:226
  31.9 4.7 %all-to-all-start = ((bf16[8,256,256]{2,1,0:T(8,128)(2,1)}), bf16[8,256,256]{2,1,0:T(8,128)(2,1)S(1)}, u32[]{:S(2)}, u32[]{:S(2)}) async-start(bf16[8,256,256]{2,1,0:T(8,128)(2,1)} %broadcast_in_dim.15), calls=%async_computation | async-start | bytes 2097152 | tf_op jit(solution)/shard_map/all_to_all | solution.py:233
  36.8 5.4 %project.1 = (bf16[4,16,2176]{2,1,0:T(8,128)(2,1)}, bf16[4,16,2176]{2,1,0:T(8,128)(2,1)}, bf16[4,16,2176]{2,1,0:T(8,128)(2,1)}, bf16[4,16,2176]{2,1,0:T(8,128)(2,1)}) custom-call(s32[16]{0:T(128)} %order_ref.3, bf16[16,16,1024]{2,1,0:T(8,128)(2,1)} %copy-done.7, f32[1,1024]{1,0:T(1,128)} %bitcast.4, bf16[1024,1024]{1,0:T(8,128)(2,1)} %wk_ref.1, ...), custom_call_target="tpu_custom_call" | custom-call | flops 1073741824 | bytes 6291456 | tf_op jit(solution)/shard_map/project/pallas_call | solution.py:237
  43.6 2.5 %collective-permute-start.1 = (bf16[4,16,2176]{2,1,0:T(8,128)(2,1)}, bf16[4,16,2176]{2,1,0:T(8,128)(2,1)S(1)}, u32[]{:S(2)}, u32[]{:S(2)}) collective-permute-start(bf16[4,16,2176]{2,1,0:T(8,128)(2,1)} %get-tuple-element.37), channel_id=1, source_target_pairs={{0,128},{64,192},{128,0},{192,64},{1,129},{65,193},{129,1},{193,65... | collective-permute-start | bytes 835592 | tf_op jit(solution)/shard_map/ppermute | solution.py:261
  47.2 3.6 %collective-permute-done.refs_1_ = bf16[4,16,2176]{2,1,0:T(8,128)(2,1)S(1)} collective-permute-done((bf16[4,16,2176]{2,1,0:T(8,128)(2,1)}, bf16[4,16,2176]{2,1,0:T(8,128)(2,1)S(1)}, u32[]{:S(2)}, u32[]{:S(2)}) %collective-permute-start) | collective-permute-done | bytes 278560 | tf_op jit(solution)/shard_map/ppermute | solution.py:261
  50.8 7.0 %collective-permute-done.1.refs_2_ = bf16[4,16,2176]{2,1,0:T(8,128)(2,1)S(1)} collective-permute-done((bf16[4,16,2176]{2,1,0:T(8,128)(2,1)}, bf16[4,16,2176]{2,1,0:T(8,128)(2,1)S(1)}, u32[]{:S(2)}, u32[]{:S(2)}) %collective-permute-start.1) | collective-permute-done | bytes 278560 | tf_op jit(solution)/shard_map/ppermute | solution.py:261
  59.1 6.6 %all-to-all-done.rest_0_ = bf16[8,256,256]{2,1,0:T(8,128)(2,1)S(1)} async-done(((bf16[8,256,256]{2,1,0:T(8,128)(2,1)}), bf16[8,256,256]{2,1,0:T(8,128)(2,1)S(1)}, u32[]{:S(2)}, u32[]{:S(2)}) %all-to-all-start) | async-done | bytes 1048608 | tf_op jit(solution)/shard_map/all_to_all | solution.py:233
  68.4 2.7 %collective-permute-start.12 = (bf16[4,16,2048]{2,1,0:T(8,128)(2,1)S(1)}, bf16[4,16,2048]{2,1,0:T(8,128)(2,1)S(1)}, u32[]{:S(2)}, u32[]{:S(2)}) collective-permute-start(bf16[4,16,2048]{2,1,0:T(8,128)(2,1)S(1)} %add.5.rest_0_), channel_id=1, source_target_pairs={{0,56},{8,0},{16,8},{24,16},{32,24},{40,32},{48,40},{56,48},{1,57}... | collective-permute-start | bytes 786440 | tf_op jit(solution)/shard_map/ppermute | solution.py:43
  71.1 5.4 %collective-permute-done.8.rest_1_ = bf16[4,16,2048]{2,1,0:T(8,128)(2,1)S(1)} collective-permute-done((bf16[4,16,2048]{2,1,0:T(8,128)(2,1)S(1)}, bf16[4,16,2048]{2,1,0:T(8,128)(2,1)S(1)}, u32[]{:S(2)}, u32[]{:S(2)}) %collective-permute-start.8) | collective-permute-done | bytes 262176 | tf_op jit(solution)/shard_map/ppermute | solution.py:41
  76.5 2.7 %collective-permute-start.13 = (bf16[4,16,2048]{2,1,0:T(8,128)(2,1)S(1)}, bf16[4,16,2048]{2,1,0:T(8,128)(2,1)S(1)}, u32[]{:S(2)}, u32[]{:S(2)}) collective-permute-start(bf16[4,16,2048]{2,1,0:T(8,128)(2,1)S(1)} %collective-permute-done.12.rest_7_), channel_id=1, source_target_pairs={{0,56},{8,0},{16,8},{24,16},{32,24},{40,32},{48,40},{56,48},{1,57}... | collective-permute-start | bytes 786440 | tf_op jit(solution)/shard_map/ppermute | solution.py:43
  79.2 4.6 %collective-permute-done.9.rest_2_ = bf16[4,16,2048]{2,1,0:T(8,128)(2,1)S(1)} collective-permute-done((bf16[4,16,2048]{2,1,0:T(8,128)(2,1)S(1)}, bf16[4,16,2048]{2,1,0:T(8,128)(2,1)S(1)}, u32[]{:S(2)}, u32[]{:S(2)}) %collective-permute-start.9) | collective-permute-done | bytes 262176 | tf_op jit(solution)/shard_map/ppermute | solution.py:41
  83.7 2.7 %collective-permute-start.16 = (bf16[8,256,256]{2,1,0:T(8,128)(2,1)S(1)}, bf16[8,256,256]{2,1,0:T(8,128)(2,1)S(1)}, u32[]{:S(2)}, u32[]{:S(2)}) collective-permute-start(bf16[8,256,256]{2,1,0:T(8,128)(2,1)S(1)} %all-to-all-done.rest_0_), channel_id=1, source_target_pairs={{0,1},{1,0},{2,3},{3,2},{4,5},{5,4},{6,7},{7,6},{8,9},{9,8},{10,11... | collective-permute-start | bytes 3145736 | tf_op jit(solution)/shard_map/ppermute | solution.py:281
  86.4 4.8 %collective-permute-done.3.rest_1_ = bf16[8,256,256]{2,1,0:T(8,128)(2,1)S(1)} collective-permute-done((bf16[8,256,256]{2,1,0:T(8,128)(2,1)S(1)}, bf16[8,256,256]{2,1,0:T(8,128)(2,1)S(1)}, u32[]{:S(2)}, u32[]{:S(2)}) %collective-permute-start.3) | collective-permute-done | bytes 1048608 | tf_op jit(solution)/shard_map/ppermute | solution.py:273
  92.1 3.5 %collective-permute-done.10.rest_3_ = bf16[4,16,2048]{2,1,0:T(8,128)(2,1)S(1)} collective-permute-done((bf16[4,16,2048]{2,1,0:T(8,128)(2,1)S(1)}, bf16[4,16,2048]{2,1,0:T(8,128)(2,1)S(1)}, u32[]{:S(2)}, u32[]{:S(2)}) %collective-permute-start.10) | collective-permute-done | bytes 262176 | tf_op jit(solution)/shard_map/ppermute | solution.py:41
  97.7 2.3 %collective-permute-start.17 = (bf16[8,256,256]{2,1,0:T(8,128)(2,1)S(1)}, bf16[8,256,256]{2,1,0:T(8,128)(2,1)S(1)}, u32[]{:S(2)}, u32[]{:S(2)}) collective-permute-start(bf16[8,256,256]{2,1,0:T(8,128)(2,1)S(1)} %collective-permute-done.3.rest_1_), channel_id=1, source_target_pairs={{0,1},{1,0},{2,3},{3,2},{4,5},{5,4},{6,7},{7,6},{8,9},{9,8},{10,11... | collective-permute-start | bytes 3145736 | tf_op jit(solution)/shard_map/ppermute | solution.py:281
  99.9 4.5 %collective-permute-done.11.rest_4_ = bf16[4,16,2048]{2,1,0:T(8,128)(2,1)S(1)} collective-permute-done((bf16[4,16,2048]{2,1,0:T(8,128)(2,1)S(1)}, bf16[4,16,2048]{2,1,0:T(8,128)(2,1)S(1)}, u32[]{:S(2)}, u32[]{:S(2)}) %collective-permute-start.11) | collective-permute-done | bytes 262176 | tf_op jit(solution)/shard_map/ppermute | solution.py:41
  104.4 3.2 %collective-permute-start.18 = (bf16[8,256,256]{2,1,0:T(8,128)(2,1)S(1)}, bf16[8,256,256]{2,1,0:T(8,128)(2,1)S(1)}, u32[]{:S(2)}, u32[]{:S(2)}) collective-permute-start(bf16[8,256,256]{2,1,0:T(8,128)(2,1)S(1)} %collective-permute-done.5.rest_2_), channel_id=1, source_target_pairs={{0,1},{1,0},{2,3},{3,2},{4,5},{5,4},{6,7},{7,6},{8,9},{9,8},{10,11... | collective-permute-start | bytes 3145736 | tf_op jit(solution)/shard_map/ppermute | solution.py:281
  109.2 4.5 %attend.3 = (bf16[512,1024]{1,0:T(8,128)(2,1)S(1)}, bf16[512,1024]{1,0:T(8,128)(2,1)S(1)}) custom-call(s32[16]{0:T(128)S(1)} %copy-done.5, s32[16]{0:T(128)S(1)} %copy-done.6, bf16[4,256,1024]{2,1,0:T(8,128)(2,1)S(1)} %copy-done.2, bf16[4,256,1024]{2,1,0:T(8,128)(2,1)} %collective-permute-done.7.theirs_ref, bf16[4,16,2048]{2,1,0:T(8,128)(2,1)S(1)} %add.5.rest_0_, ...), custom_call_target="tpu_custom_call" | custom-call | flops 65536 | bytes 65536 | tf_op jit(solution)/shard_map/attend/pallas_call | solution.py:296
  114.3 4.5 %attend.2 = (bf16[512,1024]{1,0:T(8,128)(2,1)S(1)}, bf16[512,1024]{1,0:T(8,128)(2,1)S(1)}) custom-call(s32[16]{0:T(128)S(1)} %copy-done.5, s32[16]{0:T(128)S(1)} %copy-done.6, bf16[4,256,1024]{2,1,0:T(8,128)(2,1)S(1)} %copy-done.2, bf16[4,256,1024]{2,1,0:T(8,128)(2,1)} %collective-permute-done.7.theirs_ref, bf16[4,16,2048]{2,1,0:T(8,128)(2,1)S(1)} %add.5.rest_0_, ...), custom_call_target="tpu_custom_call" | custom-call | flops 65536 | bytes 65536 | tf_op jit(solution)/shard_map/attend/pallas_call | solution.py:296
  119.4 2.9 %collective-permute-done.20.rest_9_ = bf16[4,256,256]{2,1,0:T(8,128)(2,1)S(1)} collective-permute-done((bf16[4,256,256]{2,1,0:T(8,128)(2,1)S(1)}, bf16[4,256,256]{2,1,0:T(8,128)(2,1)S(1)}, u32[]{:S(2)}, u32[]{:S(2)}) %collective-permute-start.20) | collective-permute-done | bytes 524320 | tf_op jit(solution)/shard_map/ppermute | solution.py:281
  122.3 7.5 %output.3 = (bf16[256,1024]{1,0:T(8,128)(2,1)S(1)}, bf16[256,1024]{1,0:T(8,128)(2,1)S(1)}, bf16[256,1024]{1,0:T(8,128)(2,1)S(1)}, bf16[256,1024]{1,0:T(8,128)(2,1)S(1)}) custom-call(s32[16]{0:T(128)S(1)} %copy-done.5, bf16[512,1024]{1,0:T(8,128)(2,1)S(1)} %get-tuple-element.53.keep_ref, bf16[512,1024]{1,0:T(8,128)(2,1)S(1)} %collective-permute-done.27.come_ref, ...), custom_call_target="tpu_custom_call" | custom-call | flops 65536 | bytes 65536 | tf_op jit(solution)/shard_map/output/pallas_call | solution.py:313
  131.4 7.5 %output.2 = (bf16[256,1024]{1,0:T(8,128)(2,1)S(1)}, bf16[256,1024]{1,0:T(8,128)(2,1)S(1)}, bf16[256,1024]{1,0:T(8,128)(2,1)S(1)}, bf16[256,1024]{1,0:T(8,128)(2,1)S(1)}) custom-call(s32[16]{0:T(128)S(1)} %copy-done.5, bf16[512,1024]{1,0:T(8,128)(2,1)S(1)} %get-tuple-element.43.keep_ref, bf16[512,1024]{1,0:T(8,128)(2,1)S(1)} %collective-permute-done.15.come_ref, ...), custom_call_target="tpu_custom_call" | custom-call | flops 65536 | bytes 65536 | tf_op jit(solution)/shard_map/output/pallas_call | solution.py:313
  140.7 2.6 %collective-permute-done.28.come_ref = bf16[256,1024]{1,0:T(8,128)(2,1)S(1)} collective-permute-done((bf16[256,1024]{1,0:T(8,128)(2,1)S(1)}, bf16[256,1024]{1,0:T(8,128)(2,1)S(1)}, u32[]{:S(2)}, u32[]{:S(2)}) %collective-permute-start.28) | collective-permute-done | bytes 524320 | tf_op jit(solution)/shard_map/ppermute | solution.py:328
  145.1 9.5 %collective-permute-done.31.come_ref = bf16[256,1024]{1,0:T(8,128)(2,1)S(1)} collective-permute-done((bf16[256,1024]{1,0:T(8,128)(2,1)S(1)}, bf16[256,1024]{1,0:T(8,128)(2,1)S(1)}, u32[]{:S(2)}, u32[]{:S(2)}) %collective-permute-start.31) | collective-permute-done | bytes 524320 | tf_op jit(solution)/shard_map/ppermute | solution.py:328
  156.3 4.4 %collective-permute-start.33 = (bf16[256,512]{1,0:T(8,128)(2,1)S(1)}, bf16[256,512]{1,0:T(8,128)(2,1)S(1)}, u32[]{:S(2)}, u32[]{:S(2)}) collective-permute-start(bf16[256,512]{1,0:T(8,128)(2,1)S(1)} %get-tuple-element.62), channel_id=1, source_target_pairs={{0,0},{2,2},{4,4},{6,6},{1,7},{3,5},{5,3},{7,1},{8,8},{10,10},{12,... | collective-permute-start | bytes 786440 | tf_op jit(solution)/shard_map/ppermute | solution.py:339
  160.8 5.1 %collective-permute-done.21.come_ref = bf16[256,1024]{1,0:T(8,128)(2,1)S(1)} collective-permute-done((bf16[256,1024]{1,0:T(8,128)(2,1)S(1)}, bf16[256,1024]{1,0:T(8,128)(2,1)S(1)}, u32[]{:S(2)}, u32[]{:S(2)}) %collective-permute-start.21) | collective-permute-done | bytes 524320 | tf_op jit(solution)/shard_map/ppermute | solution.py:328
  165.8 2.0 %collective-permute-start.30 = (bf16[256,512]{1,0:T(8,128)(2,1)S(1)}, bf16[256,512]{1,0:T(8,128)(2,1)S(1)}, u32[]{:S(2)}, u32[]{:S(2)}) collective-permute-start(bf16[256,512]{1,0:T(8,128)(2,1)S(1)} %get-tuple-element.58), channel_id=1, source_target_pairs={{0,0},{2,2},{4,4},{6,6},{1,7},{3,5},{5,3},{7,1},{8,8},{10,10},{12,... | collective-permute-start | bytes 786440 | tf_op jit(solution)/shard_map/ppermute | solution.py:339
  168.0 9.1 %collective-permute-done.24.come_ref = bf16[256,1024]{1,0:T(8,128)(2,1)S(1)} collective-permute-done((bf16[256,1024]{1,0:T(8,128)(2,1)S(1)}, bf16[256,1024]{1,0:T(8,128)(2,1)S(1)}, u32[]{:S(2)}, u32[]{:S(2)}) %collective-permute-start.24) | collective-permute-done | bytes 524320 | tf_op jit(solution)/shard_map/ppermute | solution.py:328
  178.3 4.4 %collective-permute-start.26 = (bf16[256,512]{1,0:T(8,128)(2,1)S(1)}, bf16[256,512]{1,0:T(8,128)(2,1)S(1)}, u32[]{:S(2)}, u32[]{:S(2)}) collective-permute-start(bf16[256,512]{1,0:T(8,128)(2,1)S(1)} %get-tuple-element.52), channel_id=1, source_target_pairs={{0,0},{2,2},{4,4},{6,6},{1,7},{3,5},{5,3},{7,1},{8,8},{10,10},{12,... | collective-permute-start | bytes 786440 | tf_op jit(solution)/shard_map/ppermute | solution.py:339
  182.7 2.0 %collective-permute-start.23 = (bf16[256,512]{1,0:T(8,128)(2,1)S(1)}, bf16[256,512]{1,0:T(8,128)(2,1)S(1)}, u32[]{:S(2)}, u32[]{:S(2)}) collective-permute-start(bf16[256,512]{1,0:T(8,128)(2,1)S(1)} %get-tuple-element.48), channel_id=1, source_target_pairs={{0,0},{2,2},{4,4},{6,6},{1,7},{3,5},{5,3},{7,1},{8,8},{10,10},{12,... | collective-permute-start | bytes 786440 | tf_op jit(solution)/shard_map/ppermute | solution.py:339
  186.8 3.2 %collective-permute-done.26.b_ref = bf16[256,512]{1,0:T(8,128)(2,1)S(1)} collective-permute-done((bf16[256,512]{1,0:T(8,128)(2,1)S(1)}, bf16[256,512]{1,0:T(8,128)(2,1)S(1)}, u32[]{:S(2)}, u32[]{:S(2)}) %collective-permute-start.26) | collective-permute-done | bytes 262176 | tf_op jit(solution)/shard_map/ppermute | solution.py:339
  (75 shorter events, 29.5 us)
Async XLA Ops:
  1.9 28.9 %all-to-all-start.1 = ((bf16[16,16,1024]{2,1,0:T(8,128)(2,1)}), bf16[16,16,1024]{2,1,0:T(8,128)(2,1)S(1)}, u32[]{:S(2)}, u32[]{:S(2)}) async-start(bf16[16,16,1024]{2,1,0:T(8,128)(2,1)} %bitcast.1), calls=%async_computation.1 | async-start | bytes 1048576 | tf_op jit(solution)/shard_map/all_to_all | solution.py:226
  31.9 33.9 %all-to-all-start = ((bf16[8,256,256]{2,1,0:T(8,128)(2,1)}), bf16[8,256,256]{2,1,0:T(8,128)(2,1)S(1)}, u32[]{:S(2)}, u32[]{:S(2)}) async-start(bf16[8,256,256]{2,1,0:T(8,128)(2,1)} %broadcast_in_dim.15), calls=%async_computation | async-start | bytes 2097152 | tf_op jit(solution)/shard_map/all_to_all | solution.py:233
  36.6 61.1 %collective-permute-start.7 = (bf16[4,256,1024]{2,1,0:T(8,128)(2,1)}, bf16[4,256,1024]{2,1,0:T(8,128)(2,1)}, u32[]{:S(2)}, u32[]{:S(2)}) collective-permute-start(bf16[4,256,1024]{2,1,0:T(8,128)(2,1)} %mine_ref.3), channel_id=1, source_target_pairs={{0,4},{4,0},{1,5},{5,1},{2,6},{6,2},{3,7},{7,3},{8,12},{12,8},{9,1... | collective-permute-start | bytes 6291464 | tf_op jit(solution)/shard_map/ppermute | solution.py:228
  42.3 8.5 %collective-permute-start = (bf16[4,16,2176]{2,1,0:T(8,128)(2,1)}, bf16[4,16,2176]{2,1,0:T(8,128)(2,1)S(1)}, u32[]{:S(2)}, u32[]{:S(2)}) collective-permute-start(bf16[4,16,2176]{2,1,0:T(8,128)(2,1)} %get-tuple-element.36), channel_id=1, source_target_pairs={{0,64},{64,128},{128,192},{192,0},{1,65},{65,129},{129,193},{193,1... | collective-permute-start | bytes 835592 | tf_op jit(solution)/shard_map/ppermute | solution.py:261
  43.6 14.2 %collective-permute-start.1 = (bf16[4,16,2176]{2,1,0:T(8,128)(2,1)}, bf16[4,16,2176]{2,1,0:T(8,128)(2,1)S(1)}, u32[]{:S(2)}, u32[]{:S(2)}) collective-permute-start(bf16[4,16,2176]{2,1,0:T(8,128)(2,1)} %get-tuple-element.37), channel_id=1, source_target_pairs={{0,128},{64,192},{128,0},{192,64},{1,129},{65,193},{129,1},{193,65... | collective-permute-start | bytes 835592 | tf_op jit(solution)/shard_map/ppermute | solution.py:261
  46.0 11.9 %collective-permute-start.2 = (bf16[4,16,2176]{2,1,0:T(8,128)(2,1)}, bf16[4,16,2176]{2,1,0:T(8,128)(2,1)S(1)}, u32[]{:S(2)}, u32[]{:S(2)}) collective-permute-start(bf16[4,16,2176]{2,1,0:T(8,128)(2,1)} %get-tuple-element.38), channel_id=1, source_target_pairs={{0,192},{64,0},{128,64},{192,128},{1,193},{65,1},{129,65},{193,129... | collective-permute-start | bytes 835592 | tf_op jit(solution)/shard_map/ppermute | solution.py:261
  65.7 25.4 %collective-permute-start.3 = (bf16[8,256,256]{2,1,0:T(8,128)(2,1)S(1)}, bf16[8,256,256]{2,1,0:T(8,128)(2,1)S(1)}, u32[]{:S(2)}, u32[]{:S(2)}) collective-permute-start(bf16[8,256,256]{2,1,0:T(8,128)(2,1)S(1)} %all-to-all-done.rest_0_), channel_id=1, source_target_pairs={{0,64},{64,128},{128,192},{192,0},{1,65},{65,129},{129,193},{193,1... | collective-permute-start | bytes 3145736 | tf_op jit(solution)/shard_map/ppermute | solution.py:273
  67.0 24.3 %collective-permute-start.5 = (bf16[8,256,256]{2,1,0:T(8,128)(2,1)S(1)}, bf16[8,256,256]{2,1,0:T(8,128)(2,1)S(1)}, u32[]{:S(2)}, u32[]{:S(2)}) collective-permute-start(bf16[8,256,256]{2,1,0:T(8,128)(2,1)S(1)} %all-to-all-done.rest_0_), channel_id=1, source_target_pairs={{0,192},{64,0},{128,64},{192,128},{1,193},{65,1},{129,65},{193,129... | collective-permute-start | bytes 3145736 | tf_op jit(solution)/shard_map/ppermute | solution.py:274
  68.4 8.1 %collective-permute-start.8 = (bf16[4,16,2048]{2,1,0:T(8,128)(2,1)S(1)}, bf16[4,16,2048]{2,1,0:T(8,128)(2,1)S(1)}, u32[]{:S(2)}, u32[]{:S(2)}) collective-permute-start(bf16[4,16,2048]{2,1,0:T(8,128)(2,1)S(1)} %add.5.rest_0_), channel_id=1, source_target_pairs={{0,8},{8,16},{16,24},{24,32},{32,40},{40,48},{48,56},{56,0},{1,9},... | collective-permute-start | bytes 786440 | tf_op jit(solution)/shard_map/ppermute | solution.py:41
  68.4 8.1 %collective-permute-start.12 = (bf16[4,16,2048]{2,1,0:T(8,128)(2,1)S(1)}, bf16[4,16,2048]{2,1,0:T(8,128)(2,1)S(1)}, u32[]{:S(2)}, u32[]{:S(2)}) collective-permute-start(bf16[4,16,2048]{2,1,0:T(8,128)(2,1)S(1)} %add.5.rest_0_), channel_id=1, source_target_pairs={{0,56},{8,0},{16,8},{24,16},{32,24},{40,32},{48,40},{56,48},{1,57}... | collective-permute-start | bytes 786440 | tf_op jit(solution)/shard_map/ppermute | solution.py:43
  76.5 9.9 %collective-permute-start.13 = (bf16[4,16,2048]{2,1,0:T(8,128)(2,1)S(1)}, bf16[4,16,2048]{2,1,0:T(8,128)(2,1)S(1)}, u32[]{:S(2)}, u32[]{:S(2)}) collective-permute-start(bf16[4,16,2048]{2,1,0:T(8,128)(2,1)S(1)} %collective-permute-done.12.rest_7_), channel_id=1, source_target_pairs={{0,56},{8,0},{16,8},{24,16},{32,24},{40,32},{48,40},{56,48},{1,57}... | collective-permute-start | bytes 786440 | tf_op jit(solution)/shard_map/ppermute | solution.py:43
  83.7 35.1 %collective-permute-start.16 = (bf16[8,256,256]{2,1,0:T(8,128)(2,1)S(1)}, bf16[8,256,256]{2,1,0:T(8,128)(2,1)S(1)}, u32[]{:S(2)}, u32[]{:S(2)}) collective-permute-start(bf16[8,256,256]{2,1,0:T(8,128)(2,1)S(1)} %all-to-all-done.rest_0_), channel_id=1, source_target_pairs={{0,1},{1,0},{2,3},{3,2},{4,5},{5,4},{6,7},{7,6},{8,9},{9,8},{10,11... | collective-permute-start | bytes 3145736 | tf_op jit(solution)/shard_map/ppermute | solution.py:281
  86.4 9.1 %collective-permute-start.10 = (bf16[4,16,2048]{2,1,0:T(8,128)(2,1)S(1)}, bf16[4,16,2048]{2,1,0:T(8,128)(2,1)S(1)}, u32[]{:S(2)}, u32[]{:S(2)}) collective-permute-start(bf16[4,16,2048]{2,1,0:T(8,128)(2,1)S(1)} %collective-permute-done.9.rest_2_), channel_id=1, source_target_pairs={{0,8},{8,16},{16,24},{24,32},{32,40},{40,48},{48,56},{56,0},{1,9},... | collective-permute-start | bytes 786440 | tf_op jit(solution)/shard_map/ppermute | solution.py:41
  91.2 16.3 %collective-permute-start.4 = (bf16[4,256,256]{2,1,0:T(8,128)(2,1)S(1)}, bf16[4,256,256]{2,1,0:T(8,128)(2,1)S(1)}, u32[]{:S(2)}, u32[]{:S(2)}) collective-permute-start(bf16[4,256,256]{2,1,0:T(8,128)(2,1)S(1)} %slice.8), channel_id=1, source_target_pairs={{0,64},{64,128},{128,192},{192,0},{1,65},{65,129},{129,193},{193,1... | collective-permute-start | bytes 1572872 | tf_op jit(solution)/shard_map/ppermute | solution.py:277
  95.6 18.1 %collective-permute-start.6 = (bf16[4,256,256]{2,1,0:T(8,128)(2,1)S(1)}, bf16[4,256,256]{2,1,0:T(8,128)(2,1)S(1)}, u32[]{:S(2)}, u32[]{:S(2)}) collective-permute-start(bf16[4,256,256]{2,1,0:T(8,128)(2,1)S(1)} %slice.9), channel_id=1, source_target_pairs={{0,192},{64,0},{128,64},{192,128},{1,193},{65,1},{129,65},{193,129... | collective-permute-start | bytes 1572872 | tf_op jit(solution)/shard_map/ppermute | solution.py:278
  97.7 24.7 %collective-permute-start.17 = (bf16[8,256,256]{2,1,0:T(8,128)(2,1)S(1)}, bf16[8,256,256]{2,1,0:T(8,128)(2,1)S(1)}, u32[]{:S(2)}, u32[]{:S(2)}) collective-permute-start(bf16[8,256,256]{2,1,0:T(8,128)(2,1)S(1)} %collective-permute-done.3.rest_1_), channel_id=1, source_target_pairs={{0,1},{1,0},{2,3},{3,2},{4,5},{5,4},{6,7},{7,6},{8,9},{9,8},{10,11... | collective-permute-start | bytes 3145736 | tf_op jit(solution)/shard_map/ppermute | solution.py:281
  104.4 17.9 %collective-permute-start.18 = (bf16[8,256,256]{2,1,0:T(8,128)(2,1)S(1)}, bf16[8,256,256]{2,1,0:T(8,128)(2,1)S(1)}, u32[]{:S(2)}, u32[]{:S(2)}) collective-permute-start(bf16[8,256,256]{2,1,0:T(8,128)(2,1)S(1)} %collective-permute-done.5.rest_2_), channel_id=1, source_target_pairs={{0,1},{1,0},{2,3},{3,2},{4,5},{5,4},{6,7},{7,6},{8,9},{9,8},{10,11... | collective-permute-start | bytes 3145736 | tf_op jit(solution)/shard_map/ppermute | solution.py:281
  107.6 11.4 %collective-permute-start.19 = (bf16[4,256,256]{2,1,0:T(8,128)(2,1)S(1)}, bf16[4,256,256]{2,1,0:T(8,128)(2,1)S(1)}, u32[]{:S(2)}, u32[]{:S(2)}) collective-permute-start(bf16[4,256,256]{2,1,0:T(8,128)(2,1)S(1)} %collective-permute-done.4.rest_3_), channel_id=1, source_target_pairs={{0,1},{1,0},{2,3},{3,2},{4,5},{5,4},{6,7},{7,6},{8,9},{9,8},{10,11... | collective-permute-start | bytes 1572872 | tf_op jit(solution)/shard_map/ppermute | solution.py:281
  113.7 8.6 %collective-permute-start.27 = (bf16[512,1024]{1,0:T(8,128)(2,1)S(1)}, bf16[512,1024]{1,0:T(8,128)(2,1)S(1)}, u32[]{:S(2)}, u32[]{:S(2)}) collective-permute-start(bf16[512,1024]{1,0:T(8,128)(2,1)S(1)} %get-tuple-element.54), channel_id=1, source_target_pairs={{0,1},{1,0},{2,3},{3,2},{4,5},{5,4},{6,7},{7,6},{8,9},{9,8},{10,11... | collective-permute-start | bytes 3145736 | tf_op jit(solution)/shard_map/ppermute | solution.py:312
  118.8 12.6 %collective-permute-start.15 = (bf16[512,1024]{1,0:T(8,128)(2,1)S(1)}, bf16[512,1024]{1,0:T(8,128)(2,1)S(1)}, u32[]{:S(2)}, u32[]{:S(2)}) collective-permute-start(bf16[512,1024]{1,0:T(8,128)(2,1)S(1)} %get-tuple-element.44), channel_id=1, source_target_pairs={{0,1},{1,0},{2,3},{3,2},{4,5},{5,4},{6,7},{7,6},{8,9},{9,8},{10,11... | collective-permute-start | bytes 3145736 | tf_op jit(solution)/shard_map/ppermute | solution.py:312
  129.9 13.5 %collective-permute-start.28 = (bf16[256,1024]{1,0:T(8,128)(2,1)S(1)}, bf16[256,1024]{1,0:T(8,128)(2,1)S(1)}, u32[]{:S(2)}, u32[]{:S(2)}) collective-permute-start(bf16[256,1024]{1,0:T(8,128)(2,1)S(1)} %get-tuple-element.56), channel_id=1, source_target_pairs={{0,2},{2,0},{1,3},{3,1},{4,6},{6,4},{5,7},{7,5},{8,10},{10,8},{9,1... | collective-permute-start | bytes 1572872 | tf_op jit(solution)/shard_map/ppermute | solution.py:328
  130.4 24.2 %collective-permute-start.31 = (bf16[256,1024]{1,0:T(8,128)(2,1)S(1)}, bf16[256,1024]{1,0:T(8,128)(2,1)S(1)}, u32[]{:S(2)}, u32[]{:S(2)}) collective-permute-start(bf16[256,1024]{1,0:T(8,128)(2,1)S(1)} %get-tuple-element.60), channel_id=1, source_target_pairs={{0,2},{2,0},{1,3},{3,1},{4,6},{6,4},{5,7},{7,5},{8,10},{10,8},{9,1... | collective-permute-start | bytes 1572872 | tf_op jit(solution)/shard_map/ppermute | solution.py:328
  139.0 26.9 %collective-permute-start.21 = (bf16[256,1024]{1,0:T(8,128)(2,1)S(1)}, bf16[256,1024]{1,0:T(8,128)(2,1)S(1)}, u32[]{:S(2)}, u32[]{:S(2)}) collective-permute-start(bf16[256,1024]{1,0:T(8,128)(2,1)S(1)} %get-tuple-element.46), channel_id=1, source_target_pairs={{0,2},{2,0},{1,3},{3,1},{4,6},{6,4},{5,7},{7,5},{8,10},{10,8},{9,1... | collective-permute-start | bytes 1572872 | tf_op jit(solution)/shard_map/ppermute | solution.py:328
  139.7 37.4 %collective-permute-start.24 = (bf16[256,1024]{1,0:T(8,128)(2,1)S(1)}, bf16[256,1024]{1,0:T(8,128)(2,1)S(1)}, u32[]{:S(2)}, u32[]{:S(2)}) collective-permute-start(bf16[256,1024]{1,0:T(8,128)(2,1)S(1)} %get-tuple-element.50), channel_id=1, source_target_pairs={{0,2},{2,0},{1,3},{3,1},{4,6},{6,4},{5,7},{7,5},{8,10},{10,8},{9,1... | collective-permute-start | bytes 1572872 | tf_op jit(solution)/shard_map/ppermute | solution.py:328
  143.5 34.7 %collective-permute-start.29 = (bf16[256,512]{1,0:T(8,128)(2,1)S(1)}, bf16[256,512]{1,0:T(8,128)(2,1)S(1)}, u32[]{:S(2)}, u32[]{:S(2)}) collective-permute-start(bf16[256,512]{1,0:T(8,128)(2,1)S(1)} %get-tuple-element.57), channel_id=1, source_target_pairs={{0,1},{2,3},{4,5},{6,7},{1,6},{3,4},{5,2},{7,0},{8,9},{10,11},{12,... | collective-permute-start | bytes 786440 | tf_op jit(solution)/shard_map/ppermute | solution.py:338
  154.7 23.6 %collective-permute-start.32 = (bf16[256,512]{1,0:T(8,128)(2,1)S(1)}, bf16[256,512]{1,0:T(8,128)(2,1)S(1)}, u32[]{:S(2)}, u32[]{:S(2)}) collective-permute-start(bf16[256,512]{1,0:T(8,128)(2,1)S(1)} %get-tuple-element.61), channel_id=1, source_target_pairs={{0,1},{2,3},{4,5},{6,7},{1,6},{3,4},{5,2},{7,0},{8,9},{10,11},{12,... | collective-permute-start | bytes 786440 | tf_op jit(solution)/shard_map/ppermute | solution.py:338
  156.3 26.4 %collective-permute-start.33 = (bf16[256,512]{1,0:T(8,128)(2,1)S(1)}, bf16[256,512]{1,0:T(8,128)(2,1)S(1)}, u32[]{:S(2)}, u32[]{:S(2)}) collective-permute-start(bf16[256,512]{1,0:T(8,128)(2,1)S(1)} %get-tuple-element.62), channel_id=1, source_target_pairs={{0,0},{2,2},{4,4},{6,6},{1,7},{3,5},{5,3},{7,1},{8,8},{10,10},{12,... | collective-permute-start | bytes 786440 | tf_op jit(solution)/shard_map/ppermute | solution.py:339
  165.8 20.0 %collective-permute-start.30 = (bf16[256,512]{1,0:T(8,128)(2,1)S(1)}, bf16[256,512]{1,0:T(8,128)(2,1)S(1)}, u32[]{:S(2)}, u32[]{:S(2)}) collective-permute-start(bf16[256,512]{1,0:T(8,128)(2,1)S(1)} %get-tuple-element.58), channel_id=1, source_target_pairs={{0,0},{2,2},{4,4},{6,6},{1,7},{3,5},{5,3},{7,1},{8,8},{10,10},{12,... | collective-permute-start | bytes 786440 | tf_op jit(solution)/shard_map/ppermute | solution.py:339
  177.1 13.9 %collective-permute-start.22 = (bf16[256,512]{1,0:T(8,128)(2,1)S(1)}, bf16[256,512]{1,0:T(8,128)(2,1)S(1)}, u32[]{:S(2)}, u32[]{:S(2)}) collective-permute-start(bf16[256,512]{1,0:T(8,128)(2,1)S(1)} %get-tuple-element.47), channel_id=1, source_target_pairs={{0,1},{2,3},{4,5},{6,7},{1,6},{3,4},{5,2},{7,0},{8,9},{10,11},{12,... | collective-permute-start | bytes 786440 | tf_op jit(solution)/shard_map/ppermute | solution.py:338
  178.2 8.6 %collective-permute-start.25 = (bf16[256,512]{1,0:T(8,128)(2,1)S(1)}, bf16[256,512]{1,0:T(8,128)(2,1)S(1)}, u32[]{:S(2)}, u32[]{:S(2)}) collective-permute-start(bf16[256,512]{1,0:T(8,128)(2,1)S(1)} %get-tuple-element.51), channel_id=1, source_target_pairs={{0,1},{2,3},{4,5},{6,7},{1,6},{3,4},{5,2},{7,0},{8,9},{10,11},{12,... | collective-permute-start | bytes 786440 | tf_op jit(solution)/shard_map/ppermute | solution.py:338
  178.3 11.7 %collective-permute-start.26 = (bf16[256,512]{1,0:T(8,128)(2,1)S(1)}, bf16[256,512]{1,0:T(8,128)(2,1)S(1)}, u32[]{:S(2)}, u32[]{:S(2)}) collective-permute-start(bf16[256,512]{1,0:T(8,128)(2,1)S(1)} %get-tuple-element.52), channel_id=1, source_target_pairs={{0,0},{2,2},{4,4},{6,6},{1,7},{3,5},{5,3},{7,1},{8,8},{10,10},{12,... | collective-permute-start | bytes 786440 | tf_op jit(solution)/shard_map/ppermute | solution.py:339
  182.7 10.0 %collective-permute-start.23 = (bf16[256,512]{1,0:T(8,128)(2,1)S(1)}, bf16[256,512]{1,0:T(8,128)(2,1)S(1)}, u32[]{:S(2)}, u32[]{:S(2)}) collective-permute-start(bf16[256,512]{1,0:T(8,128)(2,1)S(1)} %get-tuple-element.48), channel_id=1, source_target_pairs={{0,0},{2,2},{4,4},{6,6},{1,7},{3,5},{5,3},{7,1},{8,8},{10,10},{12,... | collective-permute-start | bytes 786440 | tf_op jit(solution)/shard_map/ppermute | solution.py:339
  (12 other events, 259.6 us)
where the time goes:
time: 194 us
  waiting for transfers between devices  92.1 us (47%)
  starting transfers between devices  61.6 us (32%)
  Pallas kernels  34.1 us (18%)
  local copies, waits for them, and re-layouts  5.62 us (3%)
    ppermute x4, waiting for transfers between devices, shards(): out_come = lax.ppermute(outs[i], 'yl', SWAP)  26.2 us
    ppermute x4, waiting for transfers between devices, ring_of(): ring[k] = lax.ppermute(ring[k - 1], 'z', rotation(count, 1))  17.9 us
    all_to_all x1, waiting for transfers between devices, shards(): pieces = lax.all_to_all(cut, SEQ, 0, 0, tiled=True)  17.1 us
    pallas_call x2, Pallas kernels, shards(): pl.pallas_call(functools.partial(output_kernel, nx, nz), name='output', o...  15.1 us
    ppermute x4, starting transfers between devices, shards(): b = lax.ppermute(b, ('yh', 'yl', 'core'), beside)  13 us
    all_to_all x1, starting transfers between devices, shards(): pieces = lax.all_to_all(cut, SEQ, 0, 0, tiled=True)  11.7 us
    ppermute x3, waiting for transfers between devices, shards(): lax.ppermute(partial[r], 'x', rotation(nx, r))  10.8 us
    pallas_call x2, Pallas kernels, shards(): pl.pallas_call(functools.partial(attend_kernel, s * batch, images, nz), n...  9 us
  transfers between devices with their start and end apart: 36, of which 18 were waited for; matrix products, arithmetic and copies ran while one was open for 0% of the time, Pallas kernels for 17%

commit v1 on v0

--- a/solution.py
+++ b/solution.py
@@ -287,7 +287,7 @@
         (h * 4 + l * 2 + 1, (1 - h) * 4 + (1 - l) * 2 + 1) for h in range(2) for l in range(2)
     ]
 
-    result = None
+    result, projected = None, []
     batch = images // 2
     for s in range(2):
         block = pl.BlockSpec((1, rows, cols), lambda i, s=s: (s * batch + i, 0, 0))
@@ -323,9 +323,12 @@
             compiler_params=PARAMS,
             cost_estimate=cost(1 << 16, 1 << 16),
         )(image_caption, keep, come, *w_mine, *w_theirs)
+        projected.append(outs)
+    for s, outs in enumerate(projected):
         for i in range(batch):
             j = s * batch + i
             out_come = lax.ppermute(outs[i], "yl", SWAP)
+            out_come = after(out_come, *((a, b) if j else projected[1][2:]))
             a, b = pl.pallas_call(
                 combine_kernel,
                 name="combine",

time: 194 us -> 184 us (0.948)
  waiting for transfers between devices: 92.1 us -> 78.5 us
  starting transfers between devices: 61.6 us -> 64.9 us
    ppermute x4, waiting for transfers between devices: 26.2 us -> 19.7 us  [shards(): out_come = lax.ppermute(outs[i], 'yl', SWAP)]
    ppermute x5, starting transfers between devices: 8.61 us -> 3.61 us  [shards(): w_theirs = [lax.ppermute(w, 'core', SWAP) for w in w_mine]]
    ppermute x4, starting transfers between devices: 13 us -> 17.7 us  [shards(): b = lax.ppermute(b, ('yh', 'yl', 'core'), beside)]
    ppermute x4, waiting for transfers between devices: 5.03 us -> 1.74 us  [shards(): b = lax.ppermute(b, ('yh', 'yl', 'core'), beside)]
    ppermute x5, waiting for transfers between devices: 2.91 us -> 0.01 us  [shards(): w_theirs = [lax.ppermute(w, 'core', SWAP) for w in w_mine]]
    ppermute x3, starting transfers between devices: 5.35 us -> 8.02 us  [ring_of(): lax.ppermute(ring[(count - k + 1) % count], 'z', rotation(count, -1))]
  transfers between devices with their start and end apart: 36 -> 36, of which waited for: 18 -> 14; matrix products, arithmetic and copies ran while one was open for 0% -> 0% of each run, Pallas kernels for 17% -> 18%
where the time goes in v1:
time: 184 us; the launch traced here: 183 us
  waiting for transfers between devices  78.5 us (43%)
  starting transfers between devices  64.9 us (35%)
  Pallas kernels  34.1 us (19%)
  local copies, waits for them, and re-layouts  5.62 us (3%)
    ppermute x4, waiting for transfers between devices, shards(): out_come = lax.ppermute(outs[i], 'yl', SWAP)  19.7 us
    ppermute x4, waiting for transfers between devices, ring_of(): ring[k] = lax.ppermute(ring[k - 1], 'z', rotation(count, 1))  17.8 us
    ppermute x4, starting transfers between devices, shards(): b = lax.ppermute(b, ('yh', 'yl', 'core'), beside)  17.7 us
    all_to_all x1, waiting for transfers between devices, shards(): pieces = lax.all_to_all(cut, SEQ, 0, 0, tiled=True)  17.1 us
    pallas_call x2, Pallas kernels, shards(): pl.pallas_call(functools.partial(output_kernel, nx, nz), name='output', o...  15.1 us
    all_to_all x1, starting transfers between devices, shards(): pieces = lax.all_to_all(cut, SEQ, 0, 0, tiled=True)  11.7 us
    ppermute x3, waiting for transfers between devices, shards(): lax.ppermute(partial[r], 'x', rotation(nx, r))  10.8 us
    pallas_call x2, Pallas kernels, shards(): pl.pallas_call(functools.partial(attend_kernel, s * batch, images, nz), n...  9 us
  transfers between devices with their start and end apart: 36, of which 14 were waited for; matrix products, arithmetic and copies ran while one was open for 0% of the time, Pallas kernels for 18%

profile of v1, /device:TPU:1, one launch (start us, length us, event | category | flops | bytes accessed | tf_op | source)
XLA Modules:
  0.0 183.4 jit_solution(4064643256402831392)
XLA Ops:
  0.0 1.9 %broadcast_in_dim.14 = bf16[8,2,16,1024]{3,2,1,0:T(8,128)(2,1)} broadcast(bf16[8,16,1024]{2,1,0:T(8,128)(2,1)} %bitcast.3), dimensions={0,2,3} | broadcast | bytes 786432 | tf_op jit(solution)/shard_map/broadcast_in_dim | solution.py:224
  1.9 11.7 %all-to-all-start.1 = ((bf16[16,16,1024]{2,1,0:T(8,128)(2,1)}), bf16[16,16,1024]{2,1,0:T(8,128)(2,1)S(1)}, u32[]{:S(2)}, u32[]{:S(2)}) async-start(bf16[16,16,1024]{2,1,0:T(8,128)(2,1)} %bitcast.1), calls=%async_computation.1 | async-start | bytes 1048576 | tf_op jit(solution)/shard_map/all_to_all | solution.py:226
  13.7 17.1 %all-to-all-done.1.pieces_ref = bf16[16,16,1024]{2,1,0:T(8,128)(2,1)S(1)} async-done(((bf16[16,16,1024]{2,1,0:T(8,128)(2,1)}), bf16[16,16,1024]{2,1,0:T(8,128)(2,1)S(1)}, u32[]{:S(2)}, u32[]{:S(2)}) %all-to-all-start.1) | async-done | bytes 524320 | tf_op jit(solution)/shard_map/all_to_all | solution.py:226
  31.9 4.7 %all-to-all-start = ((bf16[8,256,256]{2,1,0:T(8,128)(2,1)}), bf16[8,256,256]{2,1,0:T(8,128)(2,1)S(1)}, u32[]{:S(2)}, u32[]{:S(2)}) async-start(bf16[8,256,256]{2,1,0:T(8,128)(2,1)} %broadcast_in_dim.15), calls=%async_computation | async-start | bytes 2097152 | tf_op jit(solution)/shard_map/all_to_all | solution.py:233
  36.8 5.4 %project.1 = (bf16[4,16,2176]{2,1,0:T(8,128)(2,1)}, bf16[4,16,2176]{2,1,0:T(8,128)(2,1)}, bf16[4,16,2176]{2,1,0:T(8,128)(2,1)}, bf16[4,16,2176]{2,1,0:T(8,128)(2,1)}) custom-call(s32[16]{0:T(128)} %order_ref.3, bf16[16,16,1024]{2,1,0:T(8,128)(2,1)} %copy-done.7, f32[1,1024]{1,0:T(1,128)} %bitcast.4, bf16[1024,1024]{1,0:T(8,128)(2,1)} %wk_ref.1, ...), custom_call_target="tpu_custom_call" | custom-call | flops 1073741824 | bytes 6291456 | tf_op jit(solution)/shard_map/project/pallas_call | solution.py:237
  43.6 2.5 %collective-permute-start.1 = (bf16[4,16,2176]{2,1,0:T(8,128)(2,1)}, bf16[4,16,2176]{2,1,0:T(8,128)(2,1)S(1)}, u32[]{:S(2)}, u32[]{:S(2)}) collective-permute-start(bf16[4,16,2176]{2,1,0:T(8,128)(2,1)} %get-tuple-element.41), channel_id=1, source_target_pairs={{0,128},{64,192},{128,0},{192,64},{1,129},{65,193},{129,1},{193,65... | collective-permute-start | bytes 835592 | tf_op jit(solution)/shard_map/ppermute | solution.py:261
  47.2 3.6 %collective-permute-done.refs_1_ = bf16[4,16,2176]{2,1,0:T(8,128)(2,1)S(1)} collective-permute-done((bf16[4,16,2176]{2,1,0:T(8,128)(2,1)}, bf16[4,16,2176]{2,1,0:T(8,128)(2,1)S(1)}, u32[]{:S(2)}, u32[]{:S(2)}) %collective-permute-start) | collective-permute-done | bytes 278560 | tf_op jit(solution)/shard_map/ppermute | solution.py:261
  50.8 7.0 %collective-permute-done.1.refs_2_ = bf16[4,16,2176]{2,1,0:T(8,128)(2,1)S(1)} collective-permute-done((bf16[4,16,2176]{2,1,0:T(8,128)(2,1)}, bf16[4,16,2176]{2,1,0:T(8,128)(2,1)S(1)}, u32[]{:S(2)}, u32[]{:S(2)}) %collective-permute-start.1) | collective-permute-done | bytes 278560 | tf_op jit(solution)/shard_map/ppermute | solution.py:261
  59.1 6.6 %all-to-all-done.rest_0_ = bf16[8,256,256]{2,1,0:T(8,128)(2,1)S(1)} async-done(((bf16[8,256,256]{2,1,0:T(8,128)(2,1)}), bf16[8,256,256]{2,1,0:T(8,128)(2,1)S(1)}, u32[]{:S(2)}, u32[]{:S(2)}) %all-to-all-start) | async-done | bytes 1048608 | tf_op jit(solution)/shard_map/all_to_all | solution.py:233
  68.4 2.7 %collective-permute-start.12 = (bf16[4,16,2048]{2,1,0:T(8,128)(2,1)S(1)}, bf16[4,16,2048]{2,1,0:T(8,128)(2,1)S(1)}, u32[]{:S(2)}, u32[]{:S(2)}) collective-permute-start(bf16[4,16,2048]{2,1,0:T(8,128)(2,1)S(1)} %add.5.rest_0_), channel_id=1, source_target_pairs={{0,56},{8,0},{16,8},{24,16},{32,24},{40,32},{48,40},{56,48},{1,57}... | collective-permute-start | bytes 786440 | tf_op jit(solution)/shard_map/ppermute | solution.py:43
  71.1 5.4 %collective-permute-done.8.rest_1_ = bf16[4,16,2048]{2,1,0:T(8,128)(2,1)S(1)} collective-permute-done((bf16[4,16,2048]{2,1,0:T(8,128)(2,1)S(1)}, bf16[4,16,2048]{2,1,0:T(8,128)(2,1)S(1)}, u32[]{:S(2)}, u32[]{:S(2)}) %collective-permute-start.8) | collective-permute-done | bytes 262176 | tf_op jit(solution)/shard_map/ppermute | solution.py:41
  76.5 2.7 %collective-permute-start.13 = (bf16[4,16,2048]{2,1,0:T(8,128)(2,1)S(1)}, bf16[4,16,2048]{2,1,0:T(8,128)(2,1)S(1)}, u32[]{:S(2)}, u32[]{:S(2)}) collective-permute-start(bf16[4,16,2048]{2,1,0:T(8,128)(2,1)S(1)} %collective-permute-done.12.rest_7_), channel_id=1, source_target_pairs={{0,56},{8,0},{16,8},{24,16},{32,24},{40,32},{48,40},{56,48},{1,57}... | collective-permute-start | bytes 786440 | tf_op jit(solution)/shard_map/ppermute | solution.py:43
  79.2 4.6 %collective-permute-done.9.rest_2_ = bf16[4,16,2048]{2,1,0:T(8,128)(2,1)S(1)} collective-permute-done((bf16[4,16,2048]{2,1,0:T(8,128)(2,1)S(1)}, bf16[4,16,2048]{2,1,0:T(8,128)(2,1)S(1)}, u32[]{:S(2)}, u32[]{:S(2)}) %collective-permute-start.9) | collective-permute-done | bytes 262176 | tf_op jit(solution)/shard_map/ppermute | solution.py:41
  83.7 2.7 %collective-permute-start.14 = (bf16[4,16,2048]{2,1,0:T(8,128)(2,1)S(1)}, bf16[4,16,2048]{2,1,0:T(8,128)(2,1)S(1)}, u32[]{:S(2)}, u32[]{:S(2)}) collective-permute-start(bf16[4,16,2048]{2,1,0:T(8,128)(2,1)S(1)} %collective-permute-done.13.rest_6_), channel_id=1, source_target_pairs={{0,56},{8,0},{16,8},{24,16},{32,24},{40,32},{48,40},{56,48},{1,57}... | collective-permute-start | bytes 786440 | tf_op jit(solution)/shard_map/ppermute | solution.py:43
  86.4 4.8 %collective-permute-done.3.rest_1_ = bf16[8,256,256]{2,1,0:T(8,128)(2,1)S(1)} collective-permute-done((bf16[8,256,256]{2,1,0:T(8,128)(2,1)S(1)}, bf16[8,256,256]{2,1,0:T(8,128)(2,1)S(1)}, u32[]{:S(2)}, u32[]{:S(2)}) %collective-permute-start.3) | collective-permute-done | bytes 1048608 | tf_op jit(solution)/shard_map/ppermute | solution.py:273
  92.7 2.9 %collective-permute-start.6 = (bf16[4,256,256]{2,1,0:T(8,128)(2,1)S(1)}, bf16[4,256,256]{2,1,0:T(8,128)(2,1)S(1)}, u32[]{:S(2)}, u32[]{:S(2)}) collective-permute-start(bf16[4,256,256]{2,1,0:T(8,128)(2,1)S(1)} %slice.9), channel_id=1, source_target_pairs={{0,192},{64,0},{128,64},{192,128},{1,193},{65,1},{129,65},{193,129... | collective-permute-start | bytes 1572872 | tf_op jit(solution)/shard_map/ppermute | solution.py:278
  96.3 7.9 %collective-permute-done.11.rest_4_ = bf16[4,16,2048]{2,1,0:T(8,128)(2,1)S(1)} collective-permute-done((bf16[4,16,2048]{2,1,0:T(8,128)(2,1)S(1)}, bf16[4,16,2048]{2,1,0:T(8,128)(2,1)S(1)}, u32[]{:S(2)}, u32[]{:S(2)}) %collective-permute-start.11) | collective-permute-done | bytes 262176 | tf_op jit(solution)/shard_map/ppermute | solution.py:41
  105.6 1.6 copy-done.2
  107.2 4.5 %attend.3 = (bf16[512,1024]{1,0:T(8,128)(2,1)S(1)}, bf16[512,1024]{1,0:T(8,128)(2,1)S(1)}) custom-call(s32[16]{0:T(128)S(1)} %copy-done.5, s32[16]{0:T(128)S(1)} %copy-done.6, bf16[4,256,1024]{2,1,0:T(8,128)(2,1)S(1)} %copy-done.2, bf16[4,256,1024]{2,1,0:T(8,128)(2,1)} %collective-permute-done.7.theirs_ref, bf16[4,16,2048]{2,1,0:T(8,128)(2,1)S(1)} %add.5.rest_0_, ...), custom_call_target="tpu_custom_call" | custom-call | flops 65536 | bytes 65536 | tf_op jit(solution)/shard_map/attend/pallas_call | solution.py:296
  112.4 4.5 %attend.2 = (bf16[512,1024]{1,0:T(8,128)(2,1)S(1)}, bf16[512,1024]{1,0:T(8,128)(2,1)S(1)}) custom-call(s32[16]{0:T(128)S(1)} %copy-done.5, s32[16]{0:T(128)S(1)} %copy-done.6, bf16[4,256,1024]{2,1,0:T(8,128)(2,1)S(1)} %copy-done.2, bf16[4,256,1024]{2,1,0:T(8,128)(2,1)} %collective-permute-done.7.theirs_ref, bf16[4,16,2048]{2,1,0:T(8,128)(2,1)S(1)} %add.5.rest_0_, ...), custom_call_target="tpu_custom_call" | custom-call | flops 65536 | bytes 65536 | tf_op jit(solution)/shard_map/attend/pallas_call | solution.py:296
  117.4 7.5 %output.3 = (bf16[256,1024]{1,0:T(8,128)(2,1)S(1)}, bf16[256,1024]{1,0:T(8,128)(2,1)S(1)}, bf16[256,1024]{1,0:T(8,128)(2,1)S(1)}, bf16[256,1024]{1,0:T(8,128)(2,1)S(1)}) custom-call(s32[16]{0:T(128)S(1)} %copy-done.5, bf16[512,1024]{1,0:T(8,128)(2,1)S(1)} %get-tuple-element.53.keep_ref, bf16[512,1024]{1,0:T(8,128)(2,1)S(1)} %collective-permute-done.23.come_ref, ...), custom_call_target="tpu_custom_call" | custom-call | flops 65536 | bytes 65536 | tf_op jit(solution)/shard_map/output/pallas_call | solution.py:313
  126.6 7.5 %output.2 = (bf16[256,1024]{1,0:T(8,128)(2,1)S(1)}, bf16[256,1024]{1,0:T(8,128)(2,1)S(1)}, bf16[256,1024]{1,0:T(8,128)(2,1)S(1)}, bf16[256,1024]{1,0:T(8,128)(2,1)S(1)}) custom-call(s32[16]{0:T(128)S(1)} %copy-done.5, bf16[512,1024]{1,0:T(8,128)(2,1)S(1)} %get-tuple-element.47.keep_ref, bf16[512,1024]{1,0:T(8,128)(2,1)S(1)} %collective-permute-done.15.come_ref, ...), custom_call_target="tpu_custom_call" | custom-call | flops 65536 | bytes 65536 | tf_op jit(solution)/shard_map/output/pallas_call | solution.py:313
  134.1 4.5 %collective-permute-done.25.come_ref = bf16[256,1024]{1,0:T(8,128)(2,1)S(1)} collective-permute-done((bf16[256,1024]{1,0:T(8,128)(2,1)S(1)}, bf16[256,1024]{1,0:T(8,128)(2,1)S(1)}, u32[]{:S(2)}, u32[]{:S(2)}) %collective-permute-start.25) | collective-permute-done | bytes 524320 | tf_op jit(solution)/shard_map/ppermute | solution.py:330
  138.7 1.7 collective-permute-start.26
  140.4 4.4 %collective-permute-start.27 = (bf16[256,512]{1,0:T(8,128)(2,1)S(1)}, bf16[256,512]{1,0:T(8,128)(2,1)S(1)}, u32[]{:S(2)}, u32[]{:S(2)}) collective-permute-start(bf16[256,512]{1,0:T(8,128)(2,1)S(1)} %get-tuple-element.61), channel_id=1, source_target_pairs={{0,0},{2,2},{4,4},{6,6},{1,7},{3,5},{5,3},{7,1},{8,8},{10,10},{12,... | collective-permute-start | bytes 786440 | tf_op jit(solution)/shard_map/ppermute | solution.py:342
  144.9 4.9 %collective-permute-done.24.come_ref = bf16[256,1024]{1,0:T(8,128)(2,1)S(1)} collective-permute-done((bf16[256,1024]{1,0:T(8,128)(2,1)S(1)}, bf16[256,1024]{1,0:T(8,128)(2,1)S(1)}, u32[]{:S(2)}, u32[]{:S(2)}) %collective-permute-start.24) | collective-permute-done | bytes 524320 | tf_op jit(solution)/shard_map/ppermute | solution.py:330
  151.4 4.4 %collective-permute-start.29 = (bf16[256,512]{1,0:T(8,128)(2,1)S(1)}, bf16[256,512]{1,0:T(8,128)(2,1)S(1)}, u32[]{:S(2)}, u32[]{:S(2)}) collective-permute-start(bf16[256,512]{1,0:T(8,128)(2,1)S(1)} %get-tuple-element.64), channel_id=1, source_target_pairs={{0,0},{2,2},{4,4},{6,6},{1,7},{3,5},{5,3},{7,1},{8,8},{10,10},{12,... | collective-permute-start | bytes 786440 | tf_op jit(solution)/shard_map/ppermute | solution.py:342
  155.9 5.1 %collective-permute-done.22.come_ref = bf16[256,1024]{1,0:T(8,128)(2,1)S(1)} collective-permute-done((bf16[256,1024]{1,0:T(8,128)(2,1)S(1)}, bf16[256,1024]{1,0:T(8,128)(2,1)S(1)}, u32[]{:S(2)}, u32[]{:S(2)}) %collective-permute-start.22) | collective-permute-done | bytes 524320 | tf_op jit(solution)/shard_map/ppermute | solution.py:330
  162.6 4.4 %collective-permute-start.31 = (bf16[256,512]{1,0:T(8,128)(2,1)S(1)}, bf16[256,512]{1,0:T(8,128)(2,1)S(1)}, u32[]{:S(2)}, u32[]{:S(2)}) collective-permute-start(bf16[256,512]{1,0:T(8,128)(2,1)S(1)} %get-tuple-element.67), channel_id=1, source_target_pairs={{0,0},{2,2},{4,4},{6,6},{1,7},{3,5},{5,3},{7,1},{8,8},{10,10},{12,... | collective-permute-start | bytes 786440 | tf_op jit(solution)/shard_map/ppermute | solution.py:342
  167.1 5.2 %collective-permute-done.21.come_ref = bf16[256,1024]{1,0:T(8,128)(2,1)S(1)} collective-permute-done((bf16[256,1024]{1,0:T(8,128)(2,1)S(1)}, bf16[256,1024]{1,0:T(8,128)(2,1)S(1)}, u32[]{:S(2)}, u32[]{:S(2)}) %collective-permute-start.21) | collective-permute-done | bytes 524320 | tf_op jit(solution)/shard_map/ppermute | solution.py:330
  173.4 4.4 %collective-permute-start.33 = (bf16[256,512]{1,0:T(8,128)(2,1)S(1)}, bf16[256,512]{1,0:T(8,128)(2,1)S(1)}, u32[]{:S(2)}, u32[]{:S(2)}) collective-permute-start(bf16[256,512]{1,0:T(8,128)(2,1)S(1)} %get-tuple-element.70), channel_id=1, source_target_pairs={{0,0},{2,2},{4,4},{6,6},{1,7},{3,5},{5,3},{7,1},{8,8},{10,10},{12,... | collective-permute-start | bytes 786440 | tf_op jit(solution)/shard_map/ppermute | solution.py:342
  180.7 1.7 collective-permute-done.33.b_ref
  (75 shorter events, 22.8 us)
Async XLA Ops:
  1.9 28.9 %all-to-all-start.1 = ((bf16[16,16,1024]{2,1,0:T(8,128)(2,1)}), bf16[16,16,1024]{2,1,0:T(8,128)(2,1)S(1)}, u32[]{:S(2)}, u32[]{:S(2)}) async-start(bf16[16,16,1024]{2,1,0:T(8,128)(2,1)} %bitcast.1), calls=%async_computation.1 | async-start | bytes 1048576 | tf_op jit(solution)/shard_map/all_to_all | solution.py:226
  31.9 33.9 %all-to-all-start = ((bf16[8,256,256]{2,1,0:T(8,128)(2,1)}), bf16[8,256,256]{2,1,0:T(8,128)(2,1)S(1)}, u32[]{:S(2)}, u32[]{:S(2)}) async-start(bf16[8,256,256]{2,1,0:T(8,128)(2,1)} %broadcast_in_dim.15), calls=%async_computation | async-start | bytes 2097152 | tf_op jit(solution)/shard_map/all_to_all | solution.py:233
  36.6 59.1 %collective-permute-start.7 = (bf16[4,256,1024]{2,1,0:T(8,128)(2,1)}, bf16[4,256,1024]{2,1,0:T(8,128)(2,1)}, u32[]{:S(2)}, u32[]{:S(2)}) collective-permute-start(bf16[4,256,1024]{2,1,0:T(8,128)(2,1)} %mine_ref.3), channel_id=1, source_target_pairs={{0,4},{4,0},{1,5},{5,1},{2,6},{6,2},{3,7},{7,3},{8,12},{12,8},{9,1... | collective-permute-start | bytes 6291464 | tf_op jit(solution)/shard_map/ppermute | solution.py:228
  42.3 8.5 %collective-permute-start = (bf16[4,16,2176]{2,1,0:T(8,128)(2,1)}, bf16[4,16,2176]{2,1,0:T(8,128)(2,1)S(1)}, u32[]{:S(2)}, u32[]{:S(2)}) collective-permute-start(bf16[4,16,2176]{2,1,0:T(8,128)(2,1)} %get-tuple-element.40), channel_id=1, source_target_pairs={{0,64},{64,128},{128,192},{192,0},{1,65},{65,129},{129,193},{193,1... | collective-permute-start | bytes 835592 | tf_op jit(solution)/shard_map/ppermute | solution.py:261
  43.6 14.2 %collective-permute-start.1 = (bf16[4,16,2176]{2,1,0:T(8,128)(2,1)}, bf16[4,16,2176]{2,1,0:T(8,128)(2,1)S(1)}, u32[]{:S(2)}, u32[]{:S(2)}) collective-permute-start(bf16[4,16,2176]{2,1,0:T(8,128)(2,1)} %get-tuple-element.41), channel_id=1, source_target_pairs={{0,128},{64,192},{128,0},{192,64},{1,129},{65,193},{129,1},{193,65... | collective-permute-start | bytes 835592 | tf_op jit(solution)/shard_map/ppermute | solution.py:261
  46.0 11.9 %collective-permute-start.2 = (bf16[4,16,2176]{2,1,0:T(8,128)(2,1)}, bf16[4,16,2176]{2,1,0:T(8,128)(2,1)S(1)}, u32[]{:S(2)}, u32[]{:S(2)}) collective-permute-start(bf16[4,16,2176]{2,1,0:T(8,128)(2,1)} %get-tuple-element.42), channel_id=1, source_target_pairs={{0,192},{64,0},{128,64},{192,128},{1,193},{65,1},{129,65},{193,129... | collective-permute-start | bytes 835592 | tf_op jit(solution)/shard_map/ppermute | solution.py:261
  65.7 25.4 %collective-permute-start.3 = (bf16[8,256,256]{2,1,0:T(8,128)(2,1)S(1)}, bf16[8,256,256]{2,1,0:T(8,128)(2,1)S(1)}, u32[]{:S(2)}, u32[]{:S(2)}) collective-permute-start(bf16[8,256,256]{2,1,0:T(8,128)(2,1)S(1)} %all-to-all-done.rest_0_), channel_id=1, source_target_pairs={{0,64},{64,128},{128,192},{192,0},{1,65},{65,129},{129,193},{193,1... | collective-permute-start | bytes 3145736 | tf_op jit(solution)/shard_map/ppermute | solution.py:273
  67.0 25.6 %collective-permute-start.5 = (bf16[8,256,256]{2,1,0:T(8,128)(2,1)S(1)}, bf16[8,256,256]{2,1,0:T(8,128)(2,1)S(1)}, u32[]{:S(2)}, u32[]{:S(2)}) collective-permute-start(bf16[8,256,256]{2,1,0:T(8,128)(2,1)S(1)} %all-to-all-done.rest_0_), channel_id=1, source_target_pairs={{0,192},{64,0},{128,64},{192,128},{1,193},{65,1},{129,65},{193,129... | collective-permute-start | bytes 3145736 | tf_op jit(solution)/shard_map/ppermute | solution.py:274
  68.4 8.1 %collective-permute-start.8 = (bf16[4,16,2048]{2,1,0:T(8,128)(2,1)S(1)}, bf16[4,16,2048]{2,1,0:T(8,128)(2,1)S(1)}, u32[]{:S(2)}, u32[]{:S(2)}) collective-permute-start(bf16[4,16,2048]{2,1,0:T(8,128)(2,1)S(1)} %add.5.rest_0_), channel_id=1, source_target_pairs={{0,8},{8,16},{16,24},{24,32},{32,40},{40,48},{48,56},{56,0},{1,9},... | collective-permute-start | bytes 786440 | tf_op jit(solution)/shard_map/ppermute | solution.py:41
  68.4 8.1 %collective-permute-start.12 = (bf16[4,16,2048]{2,1,0:T(8,128)(2,1)S(1)}, bf16[4,16,2048]{2,1,0:T(8,128)(2,1)S(1)}, u32[]{:S(2)}, u32[]{:S(2)}) collective-permute-start(bf16[4,16,2048]{2,1,0:T(8,128)(2,1)S(1)} %add.5.rest_0_), channel_id=1, source_target_pairs={{0,56},{8,0},{16,8},{24,16},{32,24},{40,32},{48,40},{56,48},{1,57}... | collective-permute-start | bytes 786440 | tf_op jit(solution)/shard_map/ppermute | solution.py:43
  76.5 7.2 %collective-permute-start.9 = (bf16[4,16,2048]{2,1,0:T(8,128)(2,1)S(1)}, bf16[4,16,2048]{2,1,0:T(8,128)(2,1)S(1)}, u32[]{:S(2)}, u32[]{:S(2)}) collective-permute-start(bf16[4,16,2048]{2,1,0:T(8,128)(2,1)S(1)} %collective-permute-done.8.rest_1_), channel_id=1, source_target_pairs={{0,8},{8,16},{16,24},{24,32},{32,40},{40,48},{48,56},{56,0},{1,9},... | collective-permute-start | bytes 786440 | tf_op jit(solution)/shard_map/ppermute | solution.py:41
  83.7 9.0 %collective-permute-start.10 = (bf16[4,16,2048]{2,1,0:T(8,128)(2,1)S(1)}, bf16[4,16,2048]{2,1,0:T(8,128)(2,1)S(1)}, u32[]{:S(2)}, u32[]{:S(2)}) collective-permute-start(bf16[4,16,2048]{2,1,0:T(8,128)(2,1)S(1)} %collective-permute-done.9.rest_2_), channel_id=1, source_target_pairs={{0,8},{8,16},{16,24},{24,32},{32,40},{40,48},{48,56},{56,0},{1,9},... | collective-permute-start | bytes 786440 | tf_op jit(solution)/shard_map/ppermute | solution.py:41
  83.7 11.9 %collective-permute-start.14 = (bf16[4,16,2048]{2,1,0:T(8,128)(2,1)S(1)}, bf16[4,16,2048]{2,1,0:T(8,128)(2,1)S(1)}, u32[]{:S(2)}, u32[]{:S(2)}) collective-permute-start(bf16[4,16,2048]{2,1,0:T(8,128)(2,1)S(1)} %collective-permute-done.13.rest_6_), channel_id=1, source_target_pairs={{0,56},{8,0},{16,8},{24,16},{32,24},{40,32},{48,40},{56,48},{1,57}... | collective-permute-start | bytes 786440 | tf_op jit(solution)/shard_map/ppermute | solution.py:43
  91.2 21.1 %collective-permute-start.16 = (bf16[8,256,256]{2,1,0:T(8,128)(2,1)S(1)}, bf16[8,256,256]{2,1,0:T(8,128)(2,1)S(1)}, u32[]{:S(2)}, u32[]{:S(2)}) collective-permute-start(bf16[8,256,256]{2,1,0:T(8,128)(2,1)S(1)} %all-to-all-done.rest_0_), channel_id=1, source_target_pairs={{0,1},{1,0},{2,3},{3,2},{4,5},{5,4},{6,7},{7,6},{8,9},{9,8},{10,11... | collective-permute-start | bytes 3145736 | tf_op jit(solution)/shard_map/ppermute | solution.py:281
  92.6 19.1 %collective-permute-start.4 = (bf16[4,256,256]{2,1,0:T(8,128)(2,1)S(1)}, bf16[4,256,256]{2,1,0:T(8,128)(2,1)S(1)}, u32[]{:S(2)}, u32[]{:S(2)}) collective-permute-start(bf16[4,256,256]{2,1,0:T(8,128)(2,1)S(1)} %slice.8), channel_id=1, source_target_pairs={{0,64},{64,128},{128,192},{192,0},{1,65},{65,129},{129,193},{193,1... | collective-permute-start | bytes 1572872 | tf_op jit(solution)/shard_map/ppermute | solution.py:277
  92.7 19.1 %collective-permute-start.6 = (bf16[4,256,256]{2,1,0:T(8,128)(2,1)S(1)}, bf16[4,256,256]{2,1,0:T(8,128)(2,1)S(1)}, u32[]{:S(2)}, u32[]{:S(2)}) collective-permute-start(bf16[4,256,256]{2,1,0:T(8,128)(2,1)S(1)} %slice.9), channel_id=1, source_target_pairs={{0,192},{64,0},{128,64},{192,128},{1,193},{65,1},{129,65},{193,129... | collective-permute-start | bytes 1572872 | tf_op jit(solution)/shard_map/ppermute | solution.py:278
  95.6 8.5 %collective-permute-start.11 = (bf16[4,16,2048]{2,1,0:T(8,128)(2,1)S(1)}, bf16[4,16,2048]{2,1,0:T(8,128)(2,1)S(1)}, u32[]{:S(2)}, u32[]{:S(2)}) collective-permute-start(bf16[4,16,2048]{2,1,0:T(8,128)(2,1)S(1)} %collective-permute-done.10.rest_3_), channel_id=1, source_target_pairs={{0,8},{8,16},{16,24},{24,32},{32,40},{40,48},{48,56},{56,0},{1,9},... | collective-permute-start | bytes 786440 | tf_op jit(solution)/shard_map/ppermute | solution.py:41
  95.7 21.8 %collective-permute-start.17 = (bf16[8,256,256]{2,1,0:T(8,128)(2,1)S(1)}, bf16[8,256,256]{2,1,0:T(8,128)(2,1)S(1)}, u32[]{:S(2)}, u32[]{:S(2)}) collective-permute-start(bf16[8,256,256]{2,1,0:T(8,128)(2,1)S(1)} %collective-permute-done.3.rest_1_), channel_id=1, source_target_pairs={{0,1},{1,0},{2,3},{3,2},{4,5},{5,4},{6,7},{7,6},{8,9},{9,8},{10,11... | collective-permute-start | bytes 3145736 | tf_op jit(solution)/shard_map/ppermute | solution.py:281
  104.2 13.3 %collective-permute-start.18 = (bf16[8,256,256]{2,1,0:T(8,128)(2,1)S(1)}, bf16[8,256,256]{2,1,0:T(8,128)(2,1)S(1)}, u32[]{:S(2)}, u32[]{:S(2)}) collective-permute-start(bf16[8,256,256]{2,1,0:T(8,128)(2,1)S(1)} %collective-permute-done.5.rest_2_), channel_id=1, source_target_pairs={{0,1},{1,0},{2,3},{3,2},{4,5},{5,4},{6,7},{7,6},{8,9},{9,8},{10,11... | collective-permute-start | bytes 3145736 | tf_op jit(solution)/shard_map/ppermute | solution.py:281
  116.9 9.6 %collective-permute-start.15 = (bf16[512,1024]{1,0:T(8,128)(2,1)S(1)}, bf16[512,1024]{1,0:T(8,128)(2,1)S(1)}, u32[]{:S(2)}, u32[]{:S(2)}) collective-permute-start(bf16[512,1024]{1,0:T(8,128)(2,1)S(1)} %get-tuple-element.48), channel_id=1, source_target_pairs={{0,1},{1,0},{2,3},{3,2},{4,5},{5,4},{6,7},{7,6},{8,9},{9,8},{10,11... | collective-permute-start | bytes 3145736 | tf_op jit(solution)/shard_map/ppermute | solution.py:312
  125.0 13.6 %collective-permute-start.25 = (bf16[256,1024]{1,0:T(8,128)(2,1)S(1)}, bf16[256,1024]{1,0:T(8,128)(2,1)S(1)}, u32[]{:S(2)}, u32[]{:S(2)}) collective-permute-start(bf16[256,1024]{1,0:T(8,128)(2,1)S(1)} %get-tuple-element.58), channel_id=1, source_target_pairs={{0,2},{2,0},{1,3},{3,1},{4,6},{6,4},{5,7},{7,5},{8,10},{10,8},{9,1... | collective-permute-start | bytes 1572872 | tf_op jit(solution)/shard_map/ppermute | solution.py:330
  125.5 24.3 %collective-permute-start.24 = (bf16[256,1024]{1,0:T(8,128)(2,1)S(1)}, bf16[256,1024]{1,0:T(8,128)(2,1)S(1)}, u32[]{:S(2)}, u32[]{:S(2)}) collective-permute-start(bf16[256,1024]{1,0:T(8,128)(2,1)S(1)} %get-tuple-element.56), channel_id=1, source_target_pairs={{0,2},{2,0},{1,3},{3,1},{4,6},{6,4},{5,7},{7,5},{8,10},{10,8},{9,1... | collective-permute-start | bytes 1572872 | tf_op jit(solution)/shard_map/ppermute | solution.py:330
  138.7 11.1 %collective-permute-start.26 = (bf16[256,512]{1,0:T(8,128)(2,1)S(1)}, bf16[256,512]{1,0:T(8,128)(2,1)S(1)}, u32[]{:S(2)}, u32[]{:S(2)}) collective-permute-start(bf16[256,512]{1,0:T(8,128)(2,1)S(1)} %get-tuple-element.60), channel_id=1, source_target_pairs={{0,1},{2,3},{4,5},{6,7},{1,6},{3,4},{5,2},{7,0},{8,9},{10,11},{12,... | collective-permute-start | bytes 786440 | tf_op jit(solution)/shard_map/ppermute | solution.py:341
  140.4 9.4 %collective-permute-start.27 = (bf16[256,512]{1,0:T(8,128)(2,1)S(1)}, bf16[256,512]{1,0:T(8,128)(2,1)S(1)}, u32[]{:S(2)}, u32[]{:S(2)}) collective-permute-start(bf16[256,512]{1,0:T(8,128)(2,1)S(1)} %get-tuple-element.61), channel_id=1, source_target_pairs={{0,0},{2,2},{4,4},{6,6},{1,7},{3,5},{5,3},{7,1},{8,8},{10,10},{12,... | collective-permute-start | bytes 786440 | tf_op jit(solution)/shard_map/ppermute | solution.py:342
  144.8 16.2 %collective-permute-start.22 = (bf16[256,1024]{1,0:T(8,128)(2,1)S(1)}, bf16[256,1024]{1,0:T(8,128)(2,1)S(1)}, u32[]{:S(2)}, u32[]{:S(2)}) collective-permute-start(bf16[256,1024]{1,0:T(8,128)(2,1)S(1)} %get-tuple-element.52), channel_id=1, source_target_pairs={{0,2},{2,0},{1,3},{3,1},{4,6},{6,4},{5,7},{7,5},{8,10},{10,8},{9,1... | collective-permute-start | bytes 1572872 | tf_op jit(solution)/shard_map/ppermute | solution.py:330
  149.9 11.1 %collective-permute-start.28 = (bf16[256,512]{1,0:T(8,128)(2,1)S(1)}, bf16[256,512]{1,0:T(8,128)(2,1)S(1)}, u32[]{:S(2)}, u32[]{:S(2)}) collective-permute-start(bf16[256,512]{1,0:T(8,128)(2,1)S(1)} %get-tuple-element.63), channel_id=1, source_target_pairs={{0,1},{2,3},{4,5},{6,7},{1,6},{3,4},{5,2},{7,0},{8,9},{10,11},{12,... | collective-permute-start | bytes 786440 | tf_op jit(solution)/shard_map/ppermute | solution.py:341
  151.4 9.7 %collective-permute-start.29 = (bf16[256,512]{1,0:T(8,128)(2,1)S(1)}, bf16[256,512]{1,0:T(8,128)(2,1)S(1)}, u32[]{:S(2)}, u32[]{:S(2)}) collective-permute-start(bf16[256,512]{1,0:T(8,128)(2,1)S(1)} %get-tuple-element.64), channel_id=1, source_target_pairs={{0,0},{2,2},{4,4},{6,6},{1,7},{3,5},{5,3},{7,1},{8,8},{10,10},{12,... | collective-permute-start | bytes 786440 | tf_op jit(solution)/shard_map/ppermute | solution.py:342
  155.8 16.5 %collective-permute-start.21 = (bf16[256,1024]{1,0:T(8,128)(2,1)S(1)}, bf16[256,1024]{1,0:T(8,128)(2,1)S(1)}, u32[]{:S(2)}, u32[]{:S(2)}) collective-permute-start(bf16[256,1024]{1,0:T(8,128)(2,1)S(1)} %get-tuple-element.50), channel_id=1, source_target_pairs={{0,2},{2,0},{1,3},{3,1},{4,6},{6,4},{5,7},{7,5},{8,10},{10,8},{9,1... | collective-permute-start | bytes 1572872 | tf_op jit(solution)/shard_map/ppermute | solution.py:330
  161.2 11.1 %collective-permute-start.30 = (bf16[256,512]{1,0:T(8,128)(2,1)S(1)}, bf16[256,512]{1,0:T(8,128)(2,1)S(1)}, u32[]{:S(2)}, u32[]{:S(2)}) collective-permute-start(bf16[256,512]{1,0:T(8,128)(2,1)S(1)} %get-tuple-element.66), channel_id=1, source_target_pairs={{0,1},{2,3},{4,5},{6,7},{1,6},{3,4},{5,2},{7,0},{8,9},{10,11},{12,... | collective-permute-start | bytes 786440 | tf_op jit(solution)/shard_map/ppermute | solution.py:341
  162.6 9.7 %collective-permute-start.31 = (bf16[256,512]{1,0:T(8,128)(2,1)S(1)}, bf16[256,512]{1,0:T(8,128)(2,1)S(1)}, u32[]{:S(2)}, u32[]{:S(2)}) collective-permute-start(bf16[256,512]{1,0:T(8,128)(2,1)S(1)} %get-tuple-element.67), channel_id=1, source_target_pairs={{0,0},{2,2},{4,4},{6,6},{1,7},{3,5},{5,3},{7,1},{8,8},{10,10},{12,... | collective-permute-start | bytes 786440 | tf_op jit(solution)/shard_map/ppermute | solution.py:342
  172.4 8.3 %collective-permute-start.32 = (bf16[256,512]{1,0:T(8,128)(2,1)S(1)}, bf16[256,512]{1,0:T(8,128)(2,1)S(1)}, u32[]{:S(2)}, u32[]{:S(2)}) collective-permute-start(bf16[256,512]{1,0:T(8,128)(2,1)S(1)} %get-tuple-element.69), channel_id=1, source_target_pairs={{0,1},{2,3},{4,5},{6,7},{1,6},{3,4},{5,2},{7,0},{8,9},{10,11},{12,... | collective-permute-start | bytes 786440 | tf_op jit(solution)/shard_map/ppermute | solution.py:341
  173.4 9.1 %collective-permute-start.33 = (bf16[256,512]{1,0:T(8,128)(2,1)S(1)}, bf16[256,512]{1,0:T(8,128)(2,1)S(1)}, u32[]{:S(2)}, u32[]{:S(2)}) collective-permute-start(bf16[256,512]{1,0:T(8,128)(2,1)S(1)} %get-tuple-element.70), channel_id=1, source_target_pairs={{0,0},{2,2},{4,4},{6,6},{1,7},{3,5},{5,3},{7,1},{8,8},{10,10},{12,... | collective-permute-start | bytes 786440 | tf_op jit(solution)/shard_map/ppermute | solution.py:342
  (12 other events, 250.6 us)

commit v2 on v1

--- a/solution.py
+++ b/solution.py
@@ -272,13 +272,13 @@
     w_x = after(w_z, stream)
     ahead = lax.ppermute(w_x, "x", rotation(nx, 1))
     back = lax.ppermute(w_x, "x", rotation(nx, -1))
-    ring = ring_of(stream, nz, ahead, back)
+    ring = ring_of(stream, nz)
+    ahead, back = after(ahead, ring[5]), after(back, ring[5])
     far = [
         lax.ppermute(ahead[: nz // 2], "x", rotation(nx, 1)),
         lax.ppermute(back[nz // 2 :], "x", rotation(nx, -1)),
     ]
     w_mine = [w_x, ahead, back, *far]
-    w_theirs = [lax.ppermute(w, "core", SWAP) for w in w_mine]
 
     across = [(h * 4 + l * 2, h * 4 + l * 2 + 1) for h in range(2) for l in range(2)]
     across += [(h * 4 + l * 2 + 1, (1 - h) * 4 + (1 - l) * 2) for h in range(2) for l in range(2)]
@@ -303,13 +303,15 @@
             compiler_params=PARAMS,
             cost_estimate=cost(1 << 16, 1 << 16),
         )(
-            after(image_caption, *far) if s else image_caption,
+            after(image_caption, *(far if s else (ahead, back))),
             caption_lengths,
             queries,
             theirs,
             *ring,
         )
         come = lax.ppermute(send, "core", SWAP)
+        if not s:
+            w_theirs = [lax.ppermute(after(w, keep), "core", SWAP) for w in w_mine]
         outs = pl.pallas_call(
             functools.partial(output_kernel, nx, nz),
             name="output",

time: 184 us -> 183 us (level)
    ppermute x4, waiting for transfers between devices: 17.8 us -> 4.86 us  [ring_of(): ring[k] = lax.ppermute(ring[k - 1], 'z', rotation(count, 1))]
    ppermute x3, waiting for transfers between devices: 0.01 us -> 11.6 us  [ring_of(): lax.ppermute(ring[(count - k + 1) % count], 'z', rotation(count, -1))]
    ppermute x3, starting transfers between devices: 8.02 us -> 4.61 us  [ring_of(): lax.ppermute(ring[(count - k + 1) % count], 'z', rotation(count, -1))]
    ppermute x4, waiting for transfers between devices: 19.7 us -> 17.4 us  [shards(): out_come = lax.ppermute(outs[i], 'yl', SWAP)]
  transfers between devices with their start and end apart: 36 -> 36, of which waited for: 14 -> 24; matrix products, arithmetic and copies ran while one was open for 0% -> 0% of each run, Pallas kernels for 18% -> 18%
where the time goes in v2:
time: 183 us; the launch traced here: 182 us
  waiting for transfers between devices  77 us (42%)
  starting transfers between devices  65.1 us (36%)
  Pallas kernels  34.1 us (19%)
  local copies, waits for them, and re-layouts  5.63 us (3%)
    ppermute x4, starting transfers between devices, shards(): b = lax.ppermute(b, ('yh', 'yl', 'core'), beside)  18.4 us
    ppermute x4, waiting for transfers between devices, shards(): out_come = lax.ppermute(outs[i], 'yl', SWAP)  17.4 us
    all_to_all x1, waiting for transfers between devices, shards(): pieces = lax.all_to_all(cut, SEQ, 0, 0, tiled=True)  17.1 us
    pallas_call x2, Pallas kernels, shards(): pl.pallas_call(functools.partial(output_kernel, nx, nz), name='output', o...  15 us
    all_to_all x1, starting transfers between devices, shards(): pieces = lax.all_to_all(cut, SEQ, 0, 0, tiled=True)  11.7 us
    ppermute x3, waiting for transfers between devices, ring_of(): lax.ppermute(ring[(count - k + 1) % count], 'z', rotation(count, -1))  11.6 us
    ppermute x3, waiting for transfers between devices, shards(): lax.ppermute(partial[r], 'x', rotation(nx, r))  10.8 us
    pallas_call x2, Pallas kernels, shards(): pl.pallas_call(functools.partial(attend_kernel, s * batch, images, nz), n...  9 us
  transfers between devices with their start and end apart: 36, of which 24 were waited for; matrix products, arithmetic and copies ran while one was open for 0% of the time, Pallas kernels for 18%

profile of v2, /device:TPU:1, one launch (start us, length us, event | category | flops | bytes accessed | tf_op | source)
XLA Modules:
  0.0 182.0 jit_solution(9966123686409659393)
XLA Ops:
  0.0 1.9 %broadcast_in_dim.14 = bf16[8,2,16,1024]{3,2,1,0:T(8,128)(2,1)} broadcast(bf16[8,16,1024]{2,1,0:T(8,128)(2,1)} %bitcast.3), dimensions={0,2,3} | broadcast | bytes 786432 | tf_op jit(solution)/shard_map/broadcast_in_dim | solution.py:224
  1.9 11.7 %all-to-all-start.1 = ((bf16[16,16,1024]{2,1,0:T(8,128)(2,1)}), bf16[16,16,1024]{2,1,0:T(8,128)(2,1)S(1)}, u32[]{:S(2)}, u32[]{:S(2)}) async-start(bf16[16,16,1024]{2,1,0:T(8,128)(2,1)} %bitcast.1), calls=%async_computation.1 | async-start | bytes 1048576 | tf_op jit(solution)/shard_map/all_to_all | solution.py:226
  13.7 17.1 %all-to-all-done.1.pieces_ref = bf16[16,16,1024]{2,1,0:T(8,128)(2,1)S(1)} async-done(((bf16[16,16,1024]{2,1,0:T(8,128)(2,1)}), bf16[16,16,1024]{2,1,0:T(8,128)(2,1)S(1)}, u32[]{:S(2)}, u32[]{:S(2)}) %all-to-all-start.1) | async-done | bytes 524320 | tf_op jit(solution)/shard_map/all_to_all | solution.py:226
  31.9 4.7 %all-to-all-start = ((bf16[8,256,256]{2,1,0:T(8,128)(2,1)}), bf16[8,256,256]{2,1,0:T(8,128)(2,1)S(1)}, u32[]{:S(2)}, u32[]{:S(2)}) async-start(bf16[8,256,256]{2,1,0:T(8,128)(2,1)} %broadcast_in_dim.15), calls=%async_computation | async-start | bytes 2097152 | tf_op jit(solution)/shard_map/all_to_all | solution.py:233
  36.8 5.4 %project.1 = (bf16[4,16,2176]{2,1,0:T(8,128)(2,1)}, bf16[4,16,2176]{2,1,0:T(8,128)(2,1)}, bf16[4,16,2176]{2,1,0:T(8,128)(2,1)}, bf16[4,16,2176]{2,1,0:T(8,128)(2,1)}) custom-call(s32[16]{0:T(128)} %order_ref.3, bf16[16,16,1024]{2,1,0:T(8,128)(2,1)} %copy-done.7, f32[1,1024]{1,0:T(1,128)} %bitcast.4, bf16[1024,1024]{1,0:T(8,128)(2,1)} %wk_ref.1, ...), custom_call_target="tpu_custom_call" | custom-call | flops 1073741824 | bytes 6291456 | tf_op jit(solution)/shard_map/project/pallas_call | solution.py:237
  43.6 2.5 %collective-permute-start.1 = (bf16[4,16,2176]{2,1,0:T(8,128)(2,1)}, bf16[4,16,2176]{2,1,0:T(8,128)(2,1)S(1)}, u32[]{:S(2)}, u32[]{:S(2)}) collective-permute-start(bf16[4,16,2176]{2,1,0:T(8,128)(2,1)} %get-tuple-element.48), channel_id=1, source_target_pairs={{0,128},{64,192},{128,0},{192,64},{1,129},{65,193},{129,1},{193,65... | collective-permute-start | bytes 835592 | tf_op jit(solution)/shard_map/ppermute | solution.py:261
  47.2 3.6 %collective-permute-done.refs_1_ = bf16[4,16,2176]{2,1,0:T(8,128)(2,1)S(1)} collective-permute-done((bf16[4,16,2176]{2,1,0:T(8,128)(2,1)}, bf16[4,16,2176]{2,1,0:T(8,128)(2,1)S(1)}, u32[]{:S(2)}, u32[]{:S(2)}) %collective-permute-start) | collective-permute-done | bytes 278560 | tf_op jit(solution)/shard_map/ppermute | solution.py:261
  50.8 7.0 %collective-permute-done.1.refs_2_ = bf16[4,16,2176]{2,1,0:T(8,128)(2,1)S(1)} collective-permute-done((bf16[4,16,2176]{2,1,0:T(8,128)(2,1)}, bf16[4,16,2176]{2,1,0:T(8,128)(2,1)S(1)}, u32[]{:S(2)}, u32[]{:S(2)}) %collective-permute-start.1) | collective-permute-done | bytes 278560 | tf_op jit(solution)/shard_map/ppermute | solution.py:261
  59.1 6.6 %all-to-all-done.rest_0_ = bf16[8,256,256]{2,1,0:T(8,128)(2,1)S(1)} async-done(((bf16[8,256,256]{2,1,0:T(8,128)(2,1)}), bf16[8,256,256]{2,1,0:T(8,128)(2,1)S(1)}, u32[]{:S(2)}, u32[]{:S(2)}) %all-to-all-start) | async-done | bytes 1048608 | tf_op jit(solution)/shard_map/all_to_all | solution.py:233
  69.9 4.2 %collective-permute-done.4.rest_7_ = bf16[4,16,2048]{2,1,0:T(8,128)(2,1)S(1)} collective-permute-done((bf16[4,16,2048]{2,1,0:T(8,128)(2,1)S(1)}, bf16[4,16,2048]{2,1,0:T(8,128)(2,1)S(1)}, u32[]{:S(2)}, u32[]{:S(2)}) %collective-permute-start.4) | collective-permute-done | bytes 262176 | tf_op jit(solution)/shard_map/ppermute | solution.py:43
  76.5 4.0 %collective-permute-done.5.rest_6_ = bf16[4,16,2048]{2,1,0:T(8,128)(2,1)S(1)} collective-permute-done((bf16[4,16,2048]{2,1,0:T(8,128)(2,1)S(1)}, bf16[4,16,2048]{2,1,0:T(8,128)(2,1)S(1)}, u32[]{:S(2)}, u32[]{:S(2)}) %collective-permute-start.5) | collective-permute-done | bytes 262176 | tf_op jit(solution)/shard_map/ppermute | solution.py:43
  80.5 3.1 %collective-permute-start.6 = (bf16[4,16,2048]{2,1,0:T(8,128)(2,1)S(1)}, bf16[4,16,2048]{2,1,0:T(8,128)(2,1)S(1)}, u32[]{:S(2)}, u32[]{:S(2)}) collective-permute-start(bf16[4,16,2048]{2,1,0:T(8,128)(2,1)S(1)} %collective-permute-done.5.rest_6_), channel_id=1, source_target_pairs={{0,56},{8,0},{16,8},{24,16},{32,24},{40,32},{48,40},{56,48},{1,57}... | collective-permute-start | bytes 786440 | tf_op jit(solution)/shard_map/ppermute | solution.py:43
  83.7 3.4 %collective-permute-done.6.rest_5_ = bf16[4,16,2048]{2,1,0:T(8,128)(2,1)S(1)} collective-permute-done((bf16[4,16,2048]{2,1,0:T(8,128)(2,1)S(1)}, bf16[4,16,2048]{2,1,0:T(8,128)(2,1)S(1)}, u32[]{:S(2)}, u32[]{:S(2)}) %collective-permute-start.6) | collective-permute-done | bytes 262176 | tf_op jit(solution)/shard_map/ppermute | solution.py:43
  87.1 4.1 %collective-permute-done.3.rest_1_ = bf16[8,256,256]{2,1,0:T(8,128)(2,1)S(1)} collective-permute-done((bf16[8,256,256]{2,1,0:T(8,128)(2,1)S(1)}, bf16[8,256,256]{2,1,0:T(8,128)(2,1)S(1)}, u32[]{:S(2)}, u32[]{:S(2)}) %collective-permute-start.3) | collective-permute-done | bytes 1048608 | tf_op jit(solution)/shard_map/ppermute | solution.py:273
  91.5 2.8 %collective-permute-start.9 = (bf16[4,256,256]{2,1,0:T(8,128)(2,1)S(1)}, bf16[4,256,256]{2,1,0:T(8,128)(2,1)S(1)}, u32[]{:S(2)}, u32[]{:S(2)}) collective-permute-start(bf16[4,256,256]{2,1,0:T(8,128)(2,1)S(1)} %slice.7), channel_id=1, source_target_pairs={{0,192},{64,0},{128,64},{192,128},{1,193},{65,1},{129,65},{193,129... | collective-permute-start | bytes 1572872 | tf_op jit(solution)/shard_map/ppermute | solution.py:279
  94.3 3.8 %collective-permute-done.14.rest_4_ = bf16[4,16,2048]{2,1,0:T(8,128)(2,1)S(1)} collective-permute-done((bf16[4,16,2048]{2,1,0:T(8,128)(2,1)S(1)}, bf16[4,16,2048]{2,1,0:T(8,128)(2,1)S(1)}, u32[]{:S(2)}, u32[]{:S(2)}) %collective-permute-start.14) | collective-permute-done | bytes 262176 | tf_op jit(solution)/shard_map/ppermute | solution.py:41
  99.7 4.5 %attend.3 = (bf16[512,1024]{1,0:T(8,128)(2,1)S(1)}, bf16[512,1024]{1,0:T(8,128)(2,1)S(1)}) custom-call(s32[16]{0:T(128)S(1)} %copy-done.5, s32[16]{0:T(128)S(1)} %copy-done.6, bf16[4,256,1024]{2,1,0:T(8,128)(2,1)S(1)} %copy-done.2, bf16[4,256,1024]{2,1,0:T(8,128)(2,1)} %collective-permute-done.10.theirs_ref, bf16[4,16,2048]{2,1,0:T(8,128)(2,1)S(1)} %add.5.rest_0_, ...), custom_call_target="tpu_custom_call" | custom-call | flops 65536 | bytes 65536 | tf_op jit(solution)/shard_map/attend/pallas_call | solution.py:296
  104.6 3.2 %collective-permute-start.19 = (bf16[4,256,256]{2,1,0:T(8,128)(2,1)S(1)}, bf16[4,256,256]{2,1,0:T(8,128)(2,1)S(1)}, u32[]{:S(2)}, u32[]{:S(2)}) collective-permute-start(bf16[4,256,256]{2,1,0:T(8,128)(2,1)S(1)} %collective-permute-done.7.rest_3_), channel_id=1, source_target_pairs={{0,1},{1,0},{2,3},{3,2},{4,5},{5,4},{6,7},{7,6},{8,9},{9,8},{10,11... | collective-permute-start | bytes 1572872 | tf_op jit(solution)/shard_map/ppermute | solution.py:314
  109.7 4.5 %attend.2 = (bf16[512,1024]{1,0:T(8,128)(2,1)S(1)}, bf16[512,1024]{1,0:T(8,128)(2,1)S(1)}) custom-call(s32[16]{0:T(128)S(1)} %copy-done.5, s32[16]{0:T(128)S(1)} %copy-done.6, bf16[4,256,1024]{2,1,0:T(8,128)(2,1)S(1)} %copy-done.2, bf16[4,256,1024]{2,1,0:T(8,128)(2,1)} %collective-permute-done.10.theirs_ref, bf16[4,16,2048]{2,1,0:T(8,128)(2,1)S(1)} %add.5.rest_0_, ...), custom_call_target="tpu_custom_call" | custom-call | flops 65536 | bytes 65536 | tf_op jit(solution)/shard_map/attend/pallas_call | solution.py:296
  116.1 7.5 %output.3 = (bf16[256,1024]{1,0:T(8,128)(2,1)S(1)}, bf16[256,1024]{1,0:T(8,128)(2,1)S(1)}, bf16[256,1024]{1,0:T(8,128)(2,1)S(1)}, bf16[256,1024]{1,0:T(8,128)(2,1)S(1)}) custom-call(s32[16]{0:T(128)S(1)} %copy-done.5, bf16[512,1024]{1,0:T(8,128)(2,1)S(1)} %get-tuple-element.58.keep_ref, bf16[512,1024]{1,0:T(8,128)(2,1)S(1)} %collective-permute-done.23.come_ref, ...), custom_call_target="tpu_custom_call" | custom-call | flops 65536 | bytes 65536 | tf_op jit(solution)/shard_map/output/pallas_call | solution.py:315
  125.2 7.5 %output.2 = (bf16[256,1024]{1,0:T(8,128)(2,1)S(1)}, bf16[256,1024]{1,0:T(8,128)(2,1)S(1)}, bf16[256,1024]{1,0:T(8,128)(2,1)S(1)}, bf16[256,1024]{1,0:T(8,128)(2,1)S(1)}) custom-call(s32[16]{0:T(128)S(1)} %copy-done.5, bf16[512,1024]{1,0:T(8,128)(2,1)S(1)} %get-tuple-element.55.keep_ref, bf16[512,1024]{1,0:T(8,128)(2,1)S(1)} %collective-permute-done.15.come_ref, ...), custom_call_target="tpu_custom_call" | custom-call | flops 65536 | bytes 65536 | tf_op jit(solution)/shard_map/output/pallas_call | solution.py:315
  132.7 4.1 %collective-permute-done.25.come_ref = bf16[256,1024]{1,0:T(8,128)(2,1)S(1)} collective-permute-done((bf16[256,1024]{1,0:T(8,128)(2,1)S(1)}, bf16[256,1024]{1,0:T(8,128)(2,1)S(1)}, u32[]{:S(2)}, u32[]{:S(2)}) %collective-permute-start.25) | collective-permute-done | bytes 524320 | tf_op jit(solution)/shard_map/ppermute | solution.py:332
  137.0 2.2 %collective-permute-start.26 = (bf16[256,512]{1,0:T(8,128)(2,1)S(1)}, bf16[256,512]{1,0:T(8,128)(2,1)S(1)}, u32[]{:S(2)}, u32[]{:S(2)}) collective-permute-start(bf16[256,512]{1,0:T(8,128)(2,1)S(1)} %get-tuple-element.74), channel_id=1, source_target_pairs={{0,1},{2,3},{4,5},{6,7},{1,6},{3,4},{5,2},{7,0},{8,9},{10,11},{12,... | collective-permute-start | bytes 786440 | tf_op jit(solution)/shard_map/ppermute | solution.py:343
  139.1 4.6 %collective-permute-start.27 = (bf16[256,512]{1,0:T(8,128)(2,1)S(1)}, bf16[256,512]{1,0:T(8,128)(2,1)S(1)}, u32[]{:S(2)}, u32[]{:S(2)}) collective-permute-start(bf16[256,512]{1,0:T(8,128)(2,1)S(1)} %get-tuple-element.75), channel_id=1, source_target_pairs={{0,0},{2,2},{4,4},{6,6},{1,7},{3,5},{5,3},{7,1},{8,8},{10,10},{12,... | collective-permute-start | bytes 786440 | tf_op jit(solution)/shard_map/ppermute | solution.py:344
  143.8 4.2 %collective-permute-done.24.come_ref = bf16[256,1024]{1,0:T(8,128)(2,1)S(1)} collective-permute-done((bf16[256,1024]{1,0:T(8,128)(2,1)S(1)}, bf16[256,1024]{1,0:T(8,128)(2,1)S(1)}, u32[]{:S(2)}, u32[]{:S(2)}) %collective-permute-start.24) | collective-permute-done | bytes 524320 | tf_op jit(solution)/shard_map/ppermute | solution.py:332
  150.1 4.6 %collective-permute-start.29 = (bf16[256,512]{1,0:T(8,128)(2,1)S(1)}, bf16[256,512]{1,0:T(8,128)(2,1)S(1)}, u32[]{:S(2)}, u32[]{:S(2)}) collective-permute-start(bf16[256,512]{1,0:T(8,128)(2,1)S(1)} %get-tuple-element.78), channel_id=1, source_target_pairs={{0,0},{2,2},{4,4},{6,6},{1,7},{3,5},{5,3},{7,1},{8,8},{10,10},{12,... | collective-permute-start | bytes 786440 | tf_op jit(solution)/shard_map/ppermute | solution.py:344
  154.8 4.5 %collective-permute-done.22.come_ref = bf16[256,1024]{1,0:T(8,128)(2,1)S(1)} collective-permute-done((bf16[256,1024]{1,0:T(8,128)(2,1)S(1)}, bf16[256,1024]{1,0:T(8,128)(2,1)S(1)}, u32[]{:S(2)}, u32[]{:S(2)}) %collective-permute-start.22) | collective-permute-done | bytes 524320 | tf_op jit(solution)/shard_map/ppermute | solution.py:332
  159.5 1.9 %collective-permute-start.30 = (bf16[256,512]{1,0:T(8,128)(2,1)S(1)}, bf16[256,512]{1,0:T(8,128)(2,1)S(1)}, u32[]{:S(2)}, u32[]{:S(2)}) collective-permute-start(bf16[256,512]{1,0:T(8,128)(2,1)S(1)} %get-tuple-element.80), channel_id=1, source_target_pairs={{0,1},{2,3},{4,5},{6,7},{1,6},{3,4},{5,2},{7,0},{8,9},{10,11},{12,... | collective-permute-start | bytes 786440 | tf_op jit(solution)/shard_map/ppermute | solution.py:343
  161.4 4.6 %collective-permute-start.31 = (bf16[256,512]{1,0:T(8,128)(2,1)S(1)}, bf16[256,512]{1,0:T(8,128)(2,1)S(1)}, u32[]{:S(2)}, u32[]{:S(2)}) collective-permute-start(bf16[256,512]{1,0:T(8,128)(2,1)S(1)} %get-tuple-element.81), channel_id=1, source_target_pairs={{0,0},{2,2},{4,4},{6,6},{1,7},{3,5},{5,3},{7,1},{8,8},{10,10},{12,... | collective-permute-start | bytes 786440 | tf_op jit(solution)/shard_map/ppermute | solution.py:344
  166.0 4.6 %collective-permute-done.21.come_ref = bf16[256,1024]{1,0:T(8,128)(2,1)S(1)} collective-permute-done((bf16[256,1024]{1,0:T(8,128)(2,1)S(1)}, bf16[256,1024]{1,0:T(8,128)(2,1)S(1)}, u32[]{:S(2)}, u32[]{:S(2)}) %collective-permute-start.21) | collective-permute-done | bytes 524320 | tf_op jit(solution)/shard_map/ppermute | solution.py:332
  171.8 4.6 %collective-permute-start.33 = (bf16[256,512]{1,0:T(8,128)(2,1)S(1)}, bf16[256,512]{1,0:T(8,128)(2,1)S(1)}, u32[]{:S(2)}, u32[]{:S(2)}) collective-permute-start(bf16[256,512]{1,0:T(8,128)(2,1)S(1)} %get-tuple-element.84), channel_id=1, source_target_pairs={{0,0},{2,2},{4,4},{6,6},{1,7},{3,5},{5,3},{7,1},{8,8},{10,10},{12,... | collective-permute-start | bytes 786440 | tf_op jit(solution)/shard_map/ppermute | solution.py:344
  179.3 1.7 collective-permute-done.33.b_ref
  (75 shorter events, 27.3 us)
Async XLA Ops:
  1.9 28.9 %all-to-all-start.1 = ((bf16[16,16,1024]{2,1,0:T(8,128)(2,1)}), bf16[16,16,1024]{2,1,0:T(8,128)(2,1)S(1)}, u32[]{:S(2)}, u32[]{:S(2)}) async-start(bf16[16,16,1024]{2,1,0:T(8,128)(2,1)} %bitcast.1), calls=%async_computation.1 | async-start | bytes 1048576 | tf_op jit(solution)/shard_map/all_to_all | solution.py:226
  31.9 33.9 %all-to-all-start = ((bf16[8,256,256]{2,1,0:T(8,128)(2,1)}), bf16[8,256,256]{2,1,0:T(8,128)(2,1)S(1)}, u32[]{:S(2)}, u32[]{:S(2)}) async-start(bf16[8,256,256]{2,1,0:T(8,128)(2,1)} %broadcast_in_dim.15), calls=%async_computation | async-start | bytes 2097152 | tf_op jit(solution)/shard_map/all_to_all | solution.py:233
  36.6 57.7 %collective-permute-start.10 = (bf16[4,256,1024]{2,1,0:T(8,128)(2,1)}, bf16[4,256,1024]{2,1,0:T(8,128)(2,1)}, u32[]{:S(2)}, u32[]{:S(2)}) collective-permute-start(bf16[4,256,1024]{2,1,0:T(8,128)(2,1)} %mine_ref.3), channel_id=1, source_target_pairs={{0,4},{4,0},{1,5},{5,1},{2,6},{6,2},{3,7},{7,3},{8,12},{12,8},{9,1... | collective-permute-start | bytes 6291464 | tf_op jit(solution)/shard_map/ppermute | solution.py:228
  42.3 8.5 %collective-permute-start = (bf16[4,16,2176]{2,1,0:T(8,128)(2,1)}, bf16[4,16,2176]{2,1,0:T(8,128)(2,1)S(1)}, u32[]{:S(2)}, u32[]{:S(2)}) collective-permute-start(bf16[4,16,2176]{2,1,0:T(8,128)(2,1)} %get-tuple-element.47), channel_id=1, source_target_pairs={{0,64},{64,128},{128,192},{192,0},{1,65},{65,129},{129,193},{193,1... | collective-permute-start | bytes 835592 | tf_op jit(solution)/shard_map/ppermute | solution.py:261
  43.6 14.2 %collective-permute-start.1 = (bf16[4,16,2176]{2,1,0:T(8,128)(2,1)}, bf16[4,16,2176]{2,1,0:T(8,128)(2,1)S(1)}, u32[]{:S(2)}, u32[]{:S(2)}) collective-permute-start(bf16[4,16,2176]{2,1,0:T(8,128)(2,1)} %get-tuple-element.48), channel_id=1, source_target_pairs={{0,128},{64,192},{128,0},{192,64},{1,129},{65,193},{129,1},{193,65... | collective-permute-start | bytes 835592 | tf_op jit(solution)/shard_map/ppermute | solution.py:261
  46.0 11.9 %collective-permute-start.2 = (bf16[4,16,2176]{2,1,0:T(8,128)(2,1)}, bf16[4,16,2176]{2,1,0:T(8,128)(2,1)S(1)}, u32[]{:S(2)}, u32[]{:S(2)}) collective-permute-start(bf16[4,16,2176]{2,1,0:T(8,128)(2,1)} %get-tuple-element.49), channel_id=1, source_target_pairs={{0,192},{64,0},{128,64},{192,128},{1,193},{65,1},{129,65},{193,129... | collective-permute-start | bytes 835592 | tf_op jit(solution)/shard_map/ppermute | solution.py:261
  65.7 25.4 %collective-permute-start.3 = (bf16[8,256,256]{2,1,0:T(8,128)(2,1)S(1)}, bf16[8,256,256]{2,1,0:T(8,128)(2,1)S(1)}, u32[]{:S(2)}, u32[]{:S(2)}) collective-permute-start(bf16[8,256,256]{2,1,0:T(8,128)(2,1)S(1)} %all-to-all-done.rest_0_), channel_id=1, source_target_pairs={{0,64},{64,128},{128,192},{192,0},{1,65},{65,129},{129,193},{193,1... | collective-permute-start | bytes 3145736 | tf_op jit(solution)/shard_map/ppermute | solution.py:273
  67.0 7.2 %collective-permute-start.4 = (bf16[4,16,2048]{2,1,0:T(8,128)(2,1)S(1)}, bf16[4,16,2048]{2,1,0:T(8,128)(2,1)S(1)}, u32[]{:S(2)}, u32[]{:S(2)}) collective-permute-start(bf16[4,16,2048]{2,1,0:T(8,128)(2,1)S(1)} %add.5.rest_0_), channel_id=1, source_target_pairs={{0,56},{8,0},{16,8},{24,16},{32,24},{40,32},{48,40},{56,48},{1,57}... | collective-permute-start | bytes 786440 | tf_op jit(solution)/shard_map/ppermute | solution.py:43
  67.0 24.5 %collective-permute-start.8 = (bf16[8,256,256]{2,1,0:T(8,128)(2,1)S(1)}, bf16[8,256,256]{2,1,0:T(8,128)(2,1)S(1)}, u32[]{:S(2)}, u32[]{:S(2)}) collective-permute-start(bf16[8,256,256]{2,1,0:T(8,128)(2,1)S(1)} %all-to-all-done.rest_0_), channel_id=1, source_target_pairs={{0,192},{64,0},{128,64},{192,128},{1,193},{65,1},{129,65},{193,129... | collective-permute-start | bytes 3145736 | tf_op jit(solution)/shard_map/ppermute | solution.py:274
  68.4 8.1 %collective-permute-start.11 = (bf16[4,16,2048]{2,1,0:T(8,128)(2,1)S(1)}, bf16[4,16,2048]{2,1,0:T(8,128)(2,1)S(1)}, u32[]{:S(2)}, u32[]{:S(2)}) collective-permute-start(bf16[4,16,2048]{2,1,0:T(8,128)(2,1)S(1)} %add.5.rest_0_), channel_id=1, source_target_pairs={{0,8},{8,16},{16,24},{24,32},{32,40},{40,48},{48,56},{56,0},{1,9},... | collective-permute-start | bytes 786440 | tf_op jit(solution)/shard_map/ppermute | solution.py:41
  76.5 7.2 %collective-permute-start.12 = (bf16[4,16,2048]{2,1,0:T(8,128)(2,1)S(1)}, bf16[4,16,2048]{2,1,0:T(8,128)(2,1)S(1)}, u32[]{:S(2)}, u32[]{:S(2)}) collective-permute-start(bf16[4,16,2048]{2,1,0:T(8,128)(2,1)S(1)} %collective-permute-done.11.rest_1_), channel_id=1, source_target_pairs={{0,8},{8,16},{16,24},{24,32},{32,40},{40,48},{48,56},{56,0},{1,9},... | collective-permute-start | bytes 786440 | tf_op jit(solution)/shard_map/ppermute | solution.py:41
  83.7 7.6 %collective-permute-start.13 = (bf16[4,16,2048]{2,1,0:T(8,128)(2,1)S(1)}, bf16[4,16,2048]{2,1,0:T(8,128)(2,1)S(1)}, u32[]{:S(2)}, u32[]{:S(2)}) collective-permute-start(bf16[4,16,2048]{2,1,0:T(8,128)(2,1)S(1)} %collective-permute-done.12.rest_2_), channel_id=1, source_target_pairs={{0,8},{8,16},{16,24},{24,32},{32,40},{40,48},{48,56},{56,0},{1,9},... | collective-permute-start | bytes 786440 | tf_op jit(solution)/shard_map/ppermute | solution.py:41
  91.2 13.4 %collective-permute-start.7 = (bf16[4,256,256]{2,1,0:T(8,128)(2,1)S(1)}, bf16[4,256,256]{2,1,0:T(8,128)(2,1)S(1)}, u32[]{:S(2)}, u32[]{:S(2)}) collective-permute-start(bf16[4,256,256]{2,1,0:T(8,128)(2,1)S(1)} %slice.6), channel_id=1, source_target_pairs={{0,64},{64,128},{128,192},{192,0},{1,65},{65,129},{129,193},{193,1... | collective-permute-start | bytes 1572872 | tf_op jit(solution)/shard_map/ppermute | solution.py:278
  91.3 6.8 %collective-permute-start.14 = (bf16[4,16,2048]{2,1,0:T(8,128)(2,1)S(1)}, bf16[4,16,2048]{2,1,0:T(8,128)(2,1)S(1)}, u32[]{:S(2)}, u32[]{:S(2)}) collective-permute-start(bf16[4,16,2048]{2,1,0:T(8,128)(2,1)S(1)} %collective-permute-done.13.rest_3_), channel_id=1, source_target_pairs={{0,8},{8,16},{16,24},{24,32},{32,40},{40,48},{48,56},{56,0},{1,9},... | collective-permute-start | bytes 786440 | tf_op jit(solution)/shard_map/ppermute | solution.py:41
  91.5 16.9 %collective-permute-start.9 = (bf16[4,256,256]{2,1,0:T(8,128)(2,1)S(1)}, bf16[4,256,256]{2,1,0:T(8,128)(2,1)S(1)}, u32[]{:S(2)}, u32[]{:S(2)}) collective-permute-start(bf16[4,256,256]{2,1,0:T(8,128)(2,1)S(1)} %slice.7), channel_id=1, source_target_pairs={{0,192},{64,0},{128,64},{192,128},{1,193},{65,1},{129,65},{193,129... | collective-permute-start | bytes 1572872 | tf_op jit(solution)/shard_map/ppermute | solution.py:279
  107.8 7.2 %collective-permute-start.16 = (bf16[8,256,256]{2,1,0:T(8,128)(2,1)S(1)}, bf16[8,256,256]{2,1,0:T(8,128)(2,1)S(1)}, u32[]{:S(2)}, u32[]{:S(2)}) collective-permute-start(bf16[8,256,256]{2,1,0:T(8,128)(2,1)S(1)} %all-to-all-done.rest_0_), channel_id=1, source_target_pairs={{0,1},{1,0},{2,3},{3,2},{4,5},{5,4},{6,7},{7,6},{8,9},{9,8},{10,11... | collective-permute-start | bytes 3145736 | tf_op jit(solution)/shard_map/ppermute | solution.py:314
  107.9 7.1 %collective-permute-start.17 = (bf16[8,256,256]{2,1,0:T(8,128)(2,1)S(1)}, bf16[8,256,256]{2,1,0:T(8,128)(2,1)S(1)}, u32[]{:S(2)}, u32[]{:S(2)}) collective-permute-start(bf16[8,256,256]{2,1,0:T(8,128)(2,1)S(1)} %collective-permute-done.3.rest_1_), channel_id=1, source_target_pairs={{0,1},{1,0},{2,3},{3,2},{4,5},{5,4},{6,7},{7,6},{8,9},{9,8},{10,11... | collective-permute-start | bytes 3145736 | tf_op jit(solution)/shard_map/ppermute | solution.py:314
  108.3 6.7 %collective-permute-start.18 = (bf16[8,256,256]{2,1,0:T(8,128)(2,1)S(1)}, bf16[8,256,256]{2,1,0:T(8,128)(2,1)S(1)}, u32[]{:S(2)}, u32[]{:S(2)}) collective-permute-start(bf16[8,256,256]{2,1,0:T(8,128)(2,1)S(1)} %collective-permute-done.8.rest_2_), channel_id=1, source_target_pairs={{0,1},{1,0},{2,3},{3,2},{4,5},{5,4},{6,7},{7,6},{8,9},{9,8},{10,11... | collective-permute-start | bytes 3145736 | tf_op jit(solution)/shard_map/ppermute | solution.py:314
  109.3 6.7 %collective-permute-start.23 = (bf16[512,1024]{1,0:T(8,128)(2,1)S(1)}, bf16[512,1024]{1,0:T(8,128)(2,1)S(1)}, u32[]{:S(2)}, u32[]{:S(2)}) collective-permute-start(bf16[512,1024]{1,0:T(8,128)(2,1)S(1)} %get-tuple-element.68), channel_id=1, source_target_pairs={{0,1},{1,0},{2,3},{3,2},{4,5},{5,4},{6,7},{7,6},{8,9},{9,8},{10,11... | collective-permute-start | bytes 3145736 | tf_op jit(solution)/shard_map/ppermute | solution.py:312
  114.6 10.6 %collective-permute-start.15 = (bf16[512,1024]{1,0:T(8,128)(2,1)S(1)}, bf16[512,1024]{1,0:T(8,128)(2,1)S(1)}, u32[]{:S(2)}, u32[]{:S(2)}) collective-permute-start(bf16[512,1024]{1,0:T(8,128)(2,1)S(1)} %get-tuple-element.56), channel_id=1, source_target_pairs={{0,1},{1,0},{2,3},{3,2},{4,5},{5,4},{6,7},{7,6},{8,9},{9,8},{10,11... | collective-permute-start | bytes 3145736 | tf_op jit(solution)/shard_map/ppermute | solution.py:312
  123.6 13.2 %collective-permute-start.25 = (bf16[256,1024]{1,0:T(8,128)(2,1)S(1)}, bf16[256,1024]{1,0:T(8,128)(2,1)S(1)}, u32[]{:S(2)}, u32[]{:S(2)}) collective-permute-start(bf16[256,1024]{1,0:T(8,128)(2,1)S(1)} %get-tuple-element.72), channel_id=1, source_target_pairs={{0,2},{2,0},{1,3},{3,1},{4,6},{6,4},{5,7},{7,5},{8,10},{10,8},{9,1... | collective-permute-start | bytes 1572872 | tf_op jit(solution)/shard_map/ppermute | solution.py:332
  124.0 24.1 %collective-permute-start.24 = (bf16[256,1024]{1,0:T(8,128)(2,1)S(1)}, bf16[256,1024]{1,0:T(8,128)(2,1)S(1)}, u32[]{:S(2)}, u32[]{:S(2)}) collective-permute-start(bf16[256,1024]{1,0:T(8,128)(2,1)S(1)} %get-tuple-element.70), channel_id=1, source_target_pairs={{0,2},{2,0},{1,3},{3,1},{4,6},{6,4},{5,7},{7,5},{8,10},{10,8},{9,1... | collective-permute-start | bytes 1572872 | tf_op jit(solution)/shard_map/ppermute | solution.py:332
  137.0 11.1 %collective-permute-start.26 = (bf16[256,512]{1,0:T(8,128)(2,1)S(1)}, bf16[256,512]{1,0:T(8,128)(2,1)S(1)}, u32[]{:S(2)}, u32[]{:S(2)}) collective-permute-start(bf16[256,512]{1,0:T(8,128)(2,1)S(1)} %get-tuple-element.74), channel_id=1, source_target_pairs={{0,1},{2,3},{4,5},{6,7},{1,6},{3,4},{5,2},{7,0},{8,9},{10,11},{12,... | collective-permute-start | bytes 786440 | tf_op jit(solution)/shard_map/ppermute | solution.py:343
  139.1 9.3 %collective-permute-start.27 = (bf16[256,512]{1,0:T(8,128)(2,1)S(1)}, bf16[256,512]{1,0:T(8,128)(2,1)S(1)}, u32[]{:S(2)}, u32[]{:S(2)}) collective-permute-start(bf16[256,512]{1,0:T(8,128)(2,1)S(1)} %get-tuple-element.75), channel_id=1, source_target_pairs={{0,0},{2,2},{4,4},{6,6},{1,7},{3,5},{5,3},{7,1},{8,8},{10,10},{12,... | collective-permute-start | bytes 786440 | tf_op jit(solution)/shard_map/ppermute | solution.py:344
  143.7 15.6 %collective-permute-start.22 = (bf16[256,1024]{1,0:T(8,128)(2,1)S(1)}, bf16[256,1024]{1,0:T(8,128)(2,1)S(1)}, u32[]{:S(2)}, u32[]{:S(2)}) collective-permute-start(bf16[256,1024]{1,0:T(8,128)(2,1)S(1)} %get-tuple-element.67), channel_id=1, source_target_pairs={{0,2},{2,0},{1,3},{3,1},{4,6},{6,4},{5,7},{7,5},{8,10},{10,8},{9,1... | collective-permute-start | bytes 1572872 | tf_op jit(solution)/shard_map/ppermute | solution.py:332
  148.5 10.8 %collective-permute-start.28 = (bf16[256,512]{1,0:T(8,128)(2,1)S(1)}, bf16[256,512]{1,0:T(8,128)(2,1)S(1)}, u32[]{:S(2)}, u32[]{:S(2)}) collective-permute-start(bf16[256,512]{1,0:T(8,128)(2,1)S(1)} %get-tuple-element.77), channel_id=1, source_target_pairs={{0,1},{2,3},{4,5},{6,7},{1,6},{3,4},{5,2},{7,0},{8,9},{10,11},{12,... | collective-permute-start | bytes 786440 | tf_op jit(solution)/shard_map/ppermute | solution.py:343
  150.1 9.3 %collective-permute-start.29 = (bf16[256,512]{1,0:T(8,128)(2,1)S(1)}, bf16[256,512]{1,0:T(8,128)(2,1)S(1)}, u32[]{:S(2)}, u32[]{:S(2)}) collective-permute-start(bf16[256,512]{1,0:T(8,128)(2,1)S(1)} %get-tuple-element.78), channel_id=1, source_target_pairs={{0,0},{2,2},{4,4},{6,6},{1,7},{3,5},{5,3},{7,1},{8,8},{10,10},{12,... | collective-permute-start | bytes 786440 | tf_op jit(solution)/shard_map/ppermute | solution.py:344
  154.7 15.8 %collective-permute-start.21 = (bf16[256,1024]{1,0:T(8,128)(2,1)S(1)}, bf16[256,1024]{1,0:T(8,128)(2,1)S(1)}, u32[]{:S(2)}, u32[]{:S(2)}) collective-permute-start(bf16[256,1024]{1,0:T(8,128)(2,1)S(1)} %get-tuple-element.65), channel_id=1, source_target_pairs={{0,2},{2,0},{1,3},{3,1},{4,6},{6,4},{5,7},{7,5},{8,10},{10,8},{9,1... | collective-permute-start | bytes 1572872 | tf_op jit(solution)/shard_map/ppermute | solution.py:332
  159.5 11.0 %collective-permute-start.30 = (bf16[256,512]{1,0:T(8,128)(2,1)S(1)}, bf16[256,512]{1,0:T(8,128)(2,1)S(1)}, u32[]{:S(2)}, u32[]{:S(2)}) collective-permute-start(bf16[256,512]{1,0:T(8,128)(2,1)S(1)} %get-tuple-element.80), channel_id=1, source_target_pairs={{0,1},{2,3},{4,5},{6,7},{1,6},{3,4},{5,2},{7,0},{8,9},{10,11},{12,... | collective-permute-start | bytes 786440 | tf_op jit(solution)/shard_map/ppermute | solution.py:343
  161.4 9.3 %collective-permute-start.31 = (bf16[256,512]{1,0:T(8,128)(2,1)S(1)}, bf16[256,512]{1,0:T(8,128)(2,1)S(1)}, u32[]{:S(2)}, u32[]{:S(2)}) collective-permute-start(bf16[256,512]{1,0:T(8,128)(2,1)S(1)} %get-tuple-element.81), channel_id=1, source_target_pairs={{0,0},{2,2},{4,4},{6,6},{1,7},{3,5},{5,3},{7,1},{8,8},{10,10},{12,... | collective-permute-start | bytes 786440 | tf_op jit(solution)/shard_map/ppermute | solution.py:344
  170.8 8.6 %collective-permute-start.32 = (bf16[256,512]{1,0:T(8,128)(2,1)S(1)}, bf16[256,512]{1,0:T(8,128)(2,1)S(1)}, u32[]{:S(2)}, u32[]{:S(2)}) collective-permute-start(bf16[256,512]{1,0:T(8,128)(2,1)S(1)} %get-tuple-element.83), channel_id=1, source_target_pairs={{0,1},{2,3},{4,5},{6,7},{1,6},{3,4},{5,2},{7,0},{8,9},{10,11},{12,... | collective-permute-start | bytes 786440 | tf_op jit(solution)/shard_map/ppermute | solution.py:343
  171.8 9.3 %collective-permute-start.33 = (bf16[256,512]{1,0:T(8,128)(2,1)S(1)}, bf16[256,512]{1,0:T(8,128)(2,1)S(1)}, u32[]{:S(2)}, u32[]{:S(2)}) collective-permute-start(bf16[256,512]{1,0:T(8,128)(2,1)S(1)} %get-tuple-element.84), channel_id=1, source_target_pairs={{0,0},{2,2},{4,4},{6,6},{1,7},{3,5},{5,3},{7,1},{8,8},{10,10},{12,... | collective-permute-start | bytes 786440 | tf_op jit(solution)/shard_map/ppermute | solution.py:344
  (12 other events, 237.0 us)
